TPU v7x, 256 devices: a whole 4x4x8 slice. The times are simulated.
256 devices in a mesh: seq: 32 (over y, x, core), mp: 8 (over z).
Axes of the slice: x: 4, y: 4, z: 8, core: 2. Of those that a mesh axis runs over, the one named last changes fastest.
Arguments:
- projections: bfloat16 [3, 4096, 49152], P(None, 'mp', 'seq'), may hold values from -6 to 6
- lengths: int32 [128], replicated, may hold values from 1 to 1536, as said below
- owners: int32 [128], replicated, may hold values from 0 to 31, as said below
- offsets: int32 [128], replicated, may hold values from 0 to 32767, as said below
- short_filter: float32 [3, 256, 7], replicated, may hold values from -2 to 2
- long_filter: bfloat16 [256, 128], replicated, may hold values from -0.9 to 0.9
- skip: float32 [4096], replicated, may hold values from -4 to 4
- out_weight: bfloat16 [4096, 8192], P('seq', 'mp'), may hold values from -0.09375 to 0.09375
Outputs:
- mixed: bfloat16 [32768, 8192], P('seq', 'mp')
Inputs may be any that keep to these rules, and one draw needn't show every extreme that they name: lengths[r] is the number of tokens of request r in packing order; the lengths sum to 32768. In every draw one request is 1536 tokens long and the last request is one token long. owners never decrease along r and name every index of seq; owner o keeps its requests, in packing order, in the first rows of its block of 1536 rows of projections, and the rows after them are unused. offsets[r] is the sum of the lengths before r. The first request of owner o starts within 256 of o * 1024; in every draw some owner starts exactly 256 before that mark and the next owner exactly 256 after its own, so that owner's requests fill all 1536 rows of its block; the last owner starts exactly 256 after its mark.
All inputs are finite; a program needn't handle non-finite values.
Results may differ from a plain program's by a relative error of at most 0.0064.
Values may be sent and summed in bfloat16 or wider, within the bound.
A program may use at most 128 MiB of HBM per device.

v0:
```python
import jax
import jax.numpy as jnp
from jax import lax
from jax.sharding import PartitionSpec as P

GSIZE = 16
SHORT = 7
LONG = 128
TOK_DEV = 1024
SPILL = 256
CAP = 1536


def padded_2(cells, sides, width):
    for axis, dim in sides:
        count = lax.axis_size(axis)
        ends = count - 1
        head = lax.slice_in_dim(cells, 0, width, axis=dim)
        tail = lax.slice_in_dim(cells, cells.shape[dim] - width, cells.shape[dim], axis=dim)
        cells = jnp.concatenate(
            [
                lax.ppermute(tail, axis, [(i, (i + 1) % count) for i in range(ends)]),
                cells,
                lax.ppermute(head, axis, [((i + 1) % count, i) for i in range(ends)]),
            ],
            axis=dim,
        )
    return cells


def block_starts(lengths, total_tokens):
    begins = jnp.cumsum(lengths) - lengths
    marked = jnp.zeros((total_tokens,), jnp.int32).at[begins].max(begins)
    return lax.cummax(marked, axis=0)


def owner_spans(owners, offsets, owner_count, total_tokens):
    member = owners[None, :] == jnp.arange(owner_count, dtype=jnp.int32)[:, None]
    owner_first = jnp.min(jnp.where(member, offsets[None, :], total_tokens), axis=1)
    owner_after = jnp.concatenate([owner_first[1:], jnp.full((1,), total_tokens, jnp.int32)])
    return (owner_first, owner_after)


def short_filtering(panels, leading, position, short_taps):
    length = panels.shape[2]
    extended = jnp.concatenate([leading, panels], axis=2)
    summed = jnp.zeros(panels.shape, jnp.float32)
    for lag_step in range(SHORT):
        window = extended[:, :, SHORT - 1 - lag_step : SHORT - 1 - lag_step + length].astype(
            jnp.float32
        )
        summed = summed + jnp.where(
            lag_step <= position, short_taps[:, :, lag_step : lag_step + 1] * window, 0.0
        )
    query = summed[0].astype(jnp.bfloat16)
    product = (summed[1] * summed[2]).astype(jnp.bfloat16)
    return lax.optimization_barrier(jnp.stack([query, product]))


def long_filtering(product, leading, position, long_taps):
    channels, length = product.shape
    per_group = min(channels, GSIZE)
    group_count = channels // per_group
    blocks = length // LONG
    batch_blocks = 1
    while batch_blocks * 2 <= max(1, 64 // group_count) and blocks % (batch_blocks * 2) == 0:
        batch_blocks = batch_blocks * 2
    extended = jnp.concatenate([leading, product], axis=1)
    earlier = extended[:, :length].reshape(group_count, per_group, blocks, LONG)
    current = product.reshape(group_count, per_group, blocks, LONG)
    window = jnp.concatenate([earlier, current], axis=3)
    group_taps = long_taps.reshape(group_count, per_group, LONG)[:, 0]
    inner = jnp.arange(2 * LONG, dtype=jnp.int32)[:, None]
    outer = jnp.arange(LONG, dtype=jnp.int32)[None, :]
    lag_table = outer + LONG - inner
    picker = (lag_table[:, :, None] == jnp.arange(LONG, dtype=jnp.int32)[None, None, :]).astype(
        jnp.bfloat16
    )
    kernel = jnp.einsum(
        "ioj,gj->gio", picker, group_taps, preferred_element_type=jnp.float32
    ).astype(jnp.bfloat16)
    block_pos = position.reshape(blocks, LONG)

    def one_batch(batch_index):
        begin = batch_index * batch_blocks
        window_part = lax.dynamic_slice_in_dim(window, begin, batch_blocks, 2)
        pos_part = lax.dynamic_slice_in_dim(block_pos, begin, batch_blocks, 0)
        allowed = lag_table[None] <= pos_part[:, None, :]
        matrix = jnp.where(allowed[None], kernel[:, None], jnp.zeros((), jnp.bfloat16))
        return jnp.einsum(
            "gkbi,gbio->gkbo", window_part, matrix, preferred_element_type=jnp.float32
        )

    results = lax.map(one_batch, jnp.arange(blocks // batch_blocks, dtype=jnp.int32))
    return jnp.moveaxis(results, 0, 2).reshape(channels, length)


def gate_panels(stacked, leading, position, long_taps, gains):
    query = stacked[0]
    product = stacked[1]
    filtered = long_filtering(product, leading, position, long_taps)
    value = filtered + gains[:, None] * product.astype(jnp.float32)
    return (query.astype(jnp.float32) * value).astype(jnp.bfloat16)


def move_rows(panels, own_first, next_first, shard_start):
    panel_count = panels.shape[0]
    channels = panels.shape[1]
    margin_zeros = jnp.zeros((panel_count, channels, SPILL), panels.dtype)
    padded = jnp.concatenate([margin_zeros, panels, margin_zeros], axis=2)
    onward = lax.dynamic_slice_in_dim(padded, SPILL + shard_start + TOK_DEV - own_first, SPILL, 2)
    backward = panels[:, :, :SPILL]
    outgoing = jnp.concatenate([backward, onward], axis=2)
    framed = padded_2(outgoing, (("seq", 2),), SPILL)
    from_before = framed[:, :, :SPILL]
    from_after = framed[:, :, 3 * SPILL :]
    own_rows = lax.dynamic_slice_in_dim(padded, SPILL + shard_start - own_first, TOK_DEV, 2)
    placement = shard_start + jnp.arange(TOK_DEV, dtype=jnp.int32)
    before_rows = jnp.concatenate(
        [from_before, jnp.zeros((panel_count, channels, TOK_DEV - SPILL), panels.dtype)], axis=2
    )
    after_padded = jnp.concatenate(
        [
            jnp.zeros((panel_count, channels, TOK_DEV + SPILL), panels.dtype),
            from_after,
            margin_zeros,
        ],
        axis=2,
    )
    after_rows = lax.dynamic_slice_in_dim(
        after_padded, TOK_DEV + SPILL - (next_first - shard_start), TOK_DEV, 2
    )
    return jnp.where(
        placement < own_first, before_rows, jnp.where(placement >= next_first, after_rows, own_rows)
    )


def per_device(projections, lengths, owners, offsets, short_filter, long_filter, skip, out_weight):
    seq_count = lax.axis_size("seq")
    seq_index = lax.axis_index("seq")
    model_index = lax.axis_index("mp")
    channels = projections.shape[1]
    total_tokens = TOK_DEV * seq_count
    owner_first, owner_after = owner_spans(owners, offsets, seq_count, total_tokens)
    request_begin = block_starts(lengths, total_tokens)
    position = jnp.arange(total_tokens, dtype=jnp.int32) - request_begin
    channel_start = model_index * channels
    short_taps = lax.dynamic_slice_in_dim(
        jnp.repeat(short_filter, GSIZE, axis=1), channel_start, channels, 1
    )
    own_first = owner_first[seq_index]
    next_first = owner_after[seq_index]
    shard_start = seq_index * TOK_DEV
    padded_pos = jnp.concatenate([position, jnp.zeros((CAP,), jnp.int32)])
    owner_pos = lax.dynamic_slice_in_dim(padded_pos, own_first, CAP, 0)
    leading = jnp.zeros((3, channels, SHORT - 1), jnp.bfloat16)
    filtered = short_filtering(projections, leading, owner_pos, short_taps)
    stacked = move_rows(filtered, own_first, next_first, shard_start)
    spread_taps = jnp.repeat(long_filter, GSIZE, axis=0)
    grouped = lax.all_to_all(stacked, "seq", split_axis=1, concat_axis=2, tiled=True)
    group_width = grouped.shape[1]
    first_channel = channel_start + seq_index * group_width
    long_taps = lax.dynamic_slice_in_dim(spread_taps, first_channel, group_width, 0)
    gains = lax.dynamic_slice_in_dim(skip, first_channel, group_width, 0)
    leading_long = jnp.zeros((group_width, LONG), jnp.bfloat16)
    gated_groups = gate_panels(grouped, leading_long, position, long_taps, gains)
    gated = lax.all_to_all(gated_groups, "seq", split_axis=1, concat_axis=0, tiled=True)
    every_channel = lax.all_gather(gated, "mp", axis=0, tiled=True)
    mixed = lax.dot_general(
        every_channel,
        lax.all_gather(out_weight, "seq", axis=0, tiled=True),
        (((0,), (0,)), ((), ())),
        preferred_element_type=jnp.float32,
    )
    return mixed.astype(jnp.bfloat16)


def solution(mesh):
    placed = (P(None, "mp", "seq"), P(), P(), P(), P(), P(), P(), P("seq", "mp"))
    return jax.shard_map(
        per_device, mesh=mesh, in_specs=placed, out_specs=P("seq", "mp"), check_vma=False
    )
```

profile of v0, /device:TPU:1, one launch (start us, length us, event | category | flops | bytes accessed | tf_op | source)
XLA Modules:
  0.0 342.4 jit_solution(3282489072320257839)
XLA Ops:
  11.5 1.4 scatter_custom_fusion
  14.7 1.5 broadcast_in_dim.112
  16.2 1.8 reshape.137
  19.3 6.4 %copy.50 = bf16[3,512,1536]{2,0,1:T(4,128)(2,1)S(1)} copy(bf16[3,512,1536]{2,1,0:T(8,128)(2,1)} %param.10) | data formatting | bytes 9437184 | tf_op args[0]
  25.7 41.7 %select_add_fusion = f32[3,512,1536]{2,0,1:T(4,128)} fusion(bf16[3,512,1536]{2,0,1:T(4,128)(2,1)S(1)} %copy.50, f32[3,512]{0,1:T(8,128)S(1)} %bitcast.93, f32[3,512]{0,1:T(8,128)S(1)} %bitcast.92, f32[3,512]{0,1:T(8,128)S(1)} %bitcast.91, f32[3,512]{0,1:T(8,128)S(1)} %bitcast.97, f32[3,512]{0,1:T(8,128)S(1)} %bitcast.96, f32[3,512]{0,1:T(8,128)S(1)} %bitcast.95, ...), kind=kLoop, calls=%fused_computation.17 | loop fusion | flops 63700992 | bytes 14209536 | tf_op jit(solution)/shard_map/add | solution.py:52
  67.3 8.7 %slice.142 = bf16[1,512,1536]{2,0,1:T(2,128)(2,1)} slice(f32[3,512,1536]{2,0,1:T(4,128)} %select_add_fusion), slice={[0:1], [0:512], [0:1536]} | slice | bytes 3145728 | tf_op jit(solution)/shard_map/slice | solution.py:55
  76.0 11.5 %fusion.12 = bf16[1,512,1536]{2,0,1:T(2,128)(2,1)S(1)} fusion(f32[3,512,1536]{2,0,1:T(4,128)} %select_add_fusion), kind=kLoop, calls=%fused_computation.27 | loop fusion | flops 1572864 | bytes 7864320 | tf_op jit(solution)/shard_map/convert_element_type | solution.py:56
  87.6 7.3 %pad_maximum_fusion.1 = bf16[2,512,1536]{2,0,1:T(2,128)(2,1)S(1)} fusion(bf16[1,512,1536]{2,0,1:T(2,128)(2,1)S(1)} %fusion.12, bf16[1,512,1536]{2,0,1:T(2,128)(2,1)S(1)} %copy-done.2), kind=kLoop, calls=%fused_computation.29 | loop fusion | flops 6291456 | bytes 6291456 | tf_op jit(solution)/shard_map/stack | solution.py:57
  95.7 3.9 %pad_maximum_fusion = bf16[2,512,2048]{2,0,1:T(2,128)(2,1)S(1)} fusion(bf16[2,512,256]{2,0,1:T(2,128)(2,1)S(1)} %broadcast_in_dim.108, bf16[2,512,1536]{2,0,1:T(2,128)(2,1)S(1)} %pad_maximum_fusion.1), kind=kLoop, calls=%fused_computation.21 | loop fusion | flops 12582912 | bytes 7864320 | tf_op jit(solution)/shard_map/concatenate | solution.py:110
  99.7 2.1 constant_dynamic-slice_fusion.8
  101.7 4.4 %collective-permute-start = (bf16[2,512,256]{2,0,1:T(2,128)(2,1)}, bf16[2,512,256]{2,0,1:T(2,128)(2,1)}, u32[]{:S(2)}, u32[]{:S(2)}) collective-permute-start(bf16[2,512,256]{2,0,1:T(2,128)(2,1)} %constant_dynamic-slice_fusion.8), channel_id=1, source_target_pairs={{0,8},{8,16},{16,24},{24,32},{32,40},{40,48},{48,56},{56,64},{64,7... | collective-permute-start | bytes 1572872 | tf_op jit(solution)/shard_map/ppermute | solution.py:22
  107.3 2.6 collective-permute-start.1
  113.0 5.0 %collective-permute-done.1 = bf16[2,512,256]{2,0,1:T(2,128)(2,1)S(1)} collective-permute-done((bf16[2,512,256]{2,0,1:T(2,128)(2,1)}, bf16[2,512,256]{2,0,1:T(2,128)(2,1)S(1)}, u32[]{:S(2)}, u32[]{:S(2)}) %collective-permute-start.1) | collective-permute-done | bytes 524320 | tf_op jit(solution)/shard_map/ppermute | solution.py:24
  118.0 16.5 %broadcast_select_fusion.1 = bf16[2,512,1024]{2,0,1:T(2,128)(2,1)} fusion(pred[1024]{0:T(1024)(128)(4,1)S(1)} %get-tuple-element.129, bf16[2,512,256]{2,0,1:T(2,128)(2,1)} %collective-permute-done, bf16[2,512,2048]{2,0,1:T(2,128)(2,1)} %copy-done.3, s32[]{:T(128)S(6)} %select_n.84, s32[]{:T(128)S(6)} %select_n.83, bf16[2,512,256]{2,0,1:T(2,128)(2,1)} %copy-done.4, ...), kind=kLoop, calls=%fused_computation.23 | loop fusion | flops 8388608 | bytes 5771272 | tf_op jit(solution)/shard_map/jit(_where)/select_n | solution.py:133
  134.5 8.7 %all-to-all-start = ((bf16[2,512,1024]{2,0,1:T(2,128)(2,1)}), bf16[2,512,1024]{2,0,1:T(2,128)(2,1)}, u32[]{:S(2)}, u32[]{:S(2)}) async-start(bf16[2,512,1024]{2,0,1:T(2,128)(2,1)} %broadcast_select_fusion.1), calls=%async_computation | async-start | bytes 4194304 | tf_op jit(solution)/shard_map/all_to_all | solution.py:160
  144.4 7.4 %fusion.10 = f32[1,256,128]{2,0,1:T(1,128)S(1)} fusion(s32[256,128]{1,0:T(8,128)S(1)} %iota_subtract_fusion.1, bf16[1,16,128]{2,1,0:T(8,128)(2,1)S(1)} %dynamic-slice_bitcast_fusion), kind=kOutput, calls=%fused_computation.16 | convolution fusion | flops 12582912 | bytes 262656 | tf_op jit(solution)/shard_map/ioj,gj->gio/dot_general | solution.py:79
  151.8 19.4 %all-to-all-done = bf16[2,512,1024]{2,0,1:T(2,128)(2,1)} async-done(((bf16[2,512,1024]{2,0,1:T(2,128)(2,1)}), bf16[2,512,1024]{2,0,1:T(2,128)(2,1)}, u32[]{:S(2)}, u32[]{:S(2)}) %all-to-all-start) | async-done | bytes 2097184 | tf_op jit(solution)/shard_map/all_to_all | solution.py:160
  171.2 2.2 copy.58
  173.7 1.2 copy.75
  175.5 1.3 reshape_squeeze.3
  176.8 3.2 pad_maximum_fusion.2
  180.0 15.5 %while.11 = (s32[]{:T(128)}, f32[4,1,16,64,128]{4,2,3,1,0:T(8,128)}, s32[4]{0:T(128)S(1)}, s32[256,128]{1,0:T(8,128)S(1)}, bf16[1,256,128]{2,1,0:T(8,128)(2,1)S(...) while((s32[]{:T(128)}, ...), condition=%wide.region_7.8_spmd.clone, body=%wide.region_6.7_spmd.clone.sunk | while | flops 71335944 | bytes 2524335 | solution.py:94
  182.4 1.5 fusion.25
  186.2 1.5 fusion.25
  190.1 1.5 fusion.25
  194.0 1.5 fusion.25
  195.5 3.6 %copy.63 = f32[1,16,4,64,128]{4,3,2,1,0:T(8,128)} copy(f32[1,16,4,64,128]{4,1,3,0,2:T(8,128)} %bitcast.89) | data formatting | bytes 4194304 | tf_op jit(solution)/shard_map/transpose | solution.py:95
  199.1 2.7 reshape.142
  201.8 2.9 fusion.16
  204.7 23.0 %all_to_all.31 = bf16[16,32,1024]{2,0,1:T(8,128)(2,1)} all-to-all(bf16[16,32,1024]{2,0,1:T(8,128)(2,1)S(1)} %fusion.16), channel_id=1, replica_groups=mesh['seq'=32,'mp'=8] {'seq'}, dimensions={1} | all-to-all | bytes 2097152 | tf_op jit(solution)/shard_map/all_to_all | solution.py:167
  227.8 93.1 %all-gather.3.cloned.1.call-done = bf16[4096,1024]{1,0:T(8,128)(2,1)} async-done(((bf16[512,1024]{1,0:T(8,128)(2,1)}), bf16[4096,1024]{1,0:T(8,128)(2,1)}) %all-gather.3.cloned.1.call-update) | async-done | bytes 8388624 | tf_op jit(solution)/shard_map/all_gather | solution.py:168
  320.9 14.7 %convolution_convert_fusion = bf16[1024,1024]{1,0:T(8,128)(2,1)} fusion(bf16[4096,1024]{1,0:T(8,128)(2,1)} %all-gather.3.cloned.1.call-done, bf16[4096,1024]{1,0:T(8,128)(2,1)} %all-gather.5.cloned.1.call-done), kind=kOutput, calls=%fused_computation.36 | convolution fusion | flops 8590983168 | bytes 18874368 | tf_op jit(solution)/shard_map/dot_general | solution.py:169
  (82 shorter events, 18.5 us)
Async XLA Ops:
  6.5 137.7 %copy-start = (bf16[256,128]{1,0:T(8,128)(2,1)S(1)}, bf16[256,128]{1,0:T(8,128)(2,1)}, u32[]{:S(2)}) copy-start(bf16[256,128]{1,0:T(8,128)(2,1)} %param.15) | copy-start | bytes 196612
  6.5 221.2 %all-gather.5.cloned.1.call-start = ((), (), s32[]{:S(2)}) async-start(), calls=%async_computation.3 | async-start | bytes 8650752 | tf_op jit(solution)/shard_map/all_gather | solution.py:171
  76.0 11.6 %copy-start.2 = (bf16[1,512,1536]{2,0,1:T(2,128)(2,1)S(1)}, bf16[1,512,1536]{2,0,1:T(2,128)(2,1)}, u32[]{:S(2)}) copy-start(bf16[1,512,1536]{2,0,1:T(2,128)(2,1)} %slice.142) | copy-start | bytes 4718596
  95.7 6.0 %copy-start.4 = (bf16[2,512,256]{2,0,1:T(2,128)(2,1)}, bf16[2,512,256]{2,0,1:T(2,128)(2,1)S(1)}, u32[]{:S(2)}) copy-start(bf16[2,512,256]{2,0,1:T(2,128)(2,1)S(1)} %broadcast_in_dim.108) | copy-start | bytes 1572868
  99.6 7.6 %copy-start.3 = (bf16[2,512,2048]{2,0,1:T(2,128)(2,1)}, bf16[2,512,2048]{2,0,1:T(2,128)(2,1)S(1)}, u32[]{:S(2)}) copy-start(bf16[2,512,2048]{2,0,1:T(2,128)(2,1)S(1)} %pad_maximum_fusion) | copy-start | bytes 12582916
  101.7 11.3 %collective-permute-start = (bf16[2,512,256]{2,0,1:T(2,128)(2,1)}, bf16[2,512,256]{2,0,1:T(2,128)(2,1)}, u32[]{:S(2)}, u32[]{:S(2)}) collective-permute-start(bf16[2,512,256]{2,0,1:T(2,128)(2,1)} %constant_dynamic-slice_fusion.8), channel_id=1, source_target_pairs={{0,8},{8,16},{16,24},{24,32},{32,40},{40,48},{48,56},{56,64},{64,7... | collective-permute-start | bytes 1572872 | tf_op jit(solution)/shard_map/ppermute | solution.py:22
  107.3 10.7 %collective-permute-start.1 = (bf16[2,512,256]{2,0,1:T(2,128)(2,1)}, bf16[2,512,256]{2,0,1:T(2,128)(2,1)S(1)}, u32[]{:S(2)}, u32[]{:S(2)}) collective-permute-start(bf16[2,512,256]{2,0,1:T(2,128)(2,1)} %slice.112), channel_id=1, source_target_pairs={{8,0},{16,8},{24,16},{32,24},{40,32},{48,40},{56,48},{64,56},{72,6... | collective-permute-start | bytes 1572872 | tf_op jit(solution)/shard_map/ppermute | solution.py:24
  134.5 36.6 %all-to-all-start = ((bf16[2,512,1024]{2,0,1:T(2,128)(2,1)}), bf16[2,512,1024]{2,0,1:T(2,128)(2,1)}, u32[]{:S(2)}, u32[]{:S(2)}) async-start(bf16[2,512,1024]{2,0,1:T(2,128)(2,1)} %broadcast_select_fusion.1), calls=%async_computation | async-start | bytes 4194304 | tf_op jit(solution)/shard_map/all_to_all | solution.py:160
  143.3 177.6 %all-gather.3.cloned.1.call-start = ((), (), s32[]{:S(2)}) async-start(), calls=%async_computation.2 | async-start | bytes 9437184 | tf_op jit(solution)/shard_map/all_gather | solution.py:168
  320.9 14.7 %copy-start.1 = (bf16[256,128]{1,0:T(8,128)(2,1)S(1)}, bf16[256,128]{1,0:T(8,128)(2,1)}, u32[]{:S(2)}) copy-start(bf16[256,128]{1,0:T(8,128)(2,1)} %param.15) | copy-start | bytes 196612
Sparse Core Ops, SparseCore 0:
  9.9 62.1 all-gather.4
  227.9 92.9 all-gather.2
where the time goes:
time: 343 us; the launch traced here: 342 us
  waiting for transfers between devices  118 us (34%)
  other arithmetic  92.2 us (27%)
  local copies, waits for them, and re-layouts  45.3 us (13%)
  matrix products  28.2 us (8%)
  blocking collectives  23 us (7%)
  between operations  17.2 us (5%)
  starting transfers between devices  15.8 us (5%)
    all_gather x1, waiting for transfers between devices, per_device(): every_channel = lax.all_gather(gated, 'mp', axis=0, tiled=True)  93.1 us
    add x1, other arithmetic, short_filtering(): summed + jnp.where(lag_step <= position, short_taps[:, :, lag_step:lag_st...  41.7 us
    all_to_all x1, blocking collectives, per_device(): lax.all_to_all(gated_groups, 'seq', split_axis=1, concat_axis=0, tiled=True)  23 us
    all_to_all x1, waiting for transfers between devices, per_device(): lax.all_to_all(stacked, 'seq', split_axis=1, concat_axis=2, tiled=True)  19.4 us
    select_n x1, other arithmetic, move_rows(): jnp.where(placement < own_first, before_rows, jnp.where(placement >= next...  16.5 us
    dot_general x1, matrix products, per_device(): lax.dot_general(every_channel, lax.all_gather(out_weight, 'seq', axis=0,...  14.7 us
    convert_element_type x1, other arithmetic, short_filtering(): product = (summed[1] * summed[2]).astype(jnp.bfloat16)  11.5 us
    all_to_all x1, starting transfers between devices, per_device(): lax.all_to_all(stacked, 'seq', split_axis=1, concat_axis=2, tiled=True)  8.75 us
  transfers between devices with their start and end apart: 5, of which 3 were waited for; matrix products, arithmetic and copies ran while one was open for 44% of the time, Pallas kernels for 0%

commit v1 on v0

v1 whole, which is shorter than its diff:
```python
import functools

import jax
import jax.numpy as jnp
from jax import lax
from jax.experimental import pallas as pl
from jax.experimental.pallas import tpu as pltpu
from jax.sharding import PartitionSpec as P

MESH = pl.DeviceIdType.MESH
F32 = jnp.float32
BF16 = jnp.bfloat16

GSIZE = 16
SHORT = 7
LONG = 128
TOK = 1024
SPILL = 256
CAP = 1536
TOKENS = 32768
WIDE = 128
CHUNKS = 4
GROUPS = WIDE // GSIZE
BLOCKS = CAP // LONG
REACH = 2 * SPILL


def iota(shape, dim):
    return lax.broadcasted_iota(jnp.int32, shape, dim)


def prepare(seq, model, offsets, owners, long_filter, masks, later, taps, pick, product, gated):
    off = offsets[...]
    own = owners[...]
    first = jnp.min(jnp.where(own == seq, off, TOKENS), axis=1, keepdims=True)
    after = jnp.min(jnp.where(own == seq + 1, off, TOKENS), axis=1, keepdims=True)
    column = jnp.broadcast_to(off, (LONG, LONG)).T
    inner = iota((LONG, LONG), 0)
    outer = iota((LONG, LONG), 1)
    lag = outer - inner
    for b in range(BLOCKS):
        token = first + iota((1, LONG), 1) + b * LONG
        begin = jnp.max(jnp.where(column <= token, column, 0), axis=0, keepdims=True)
        pos = token - begin
        older = (lag < 0) & (lag + LONG <= pos)
        newer = (lag >= 0) & (lag <= pos)
        masks[b, 0:LONG, :] = jnp.where(older, 1.0, 0.0).astype(BF16)
        masks[b, LONG : 2 * LONG, :] = jnp.where(newer, 1.0, 0.0).astype(BF16)
        later[:, b * LONG : (b + 1) * LONG] = jnp.broadcast_to(
            jnp.where(pos >= 1, 1.0, 0.0), (8, LONG)
        )
    rows = CHUNKS * GROUPS
    taps[...] = long_filter[pl.ds(pl.multiple_of(model * rows, rows), rows), :].astype(F32)
    shift = first - seq * TOK + SPILL
    turned = iota((SPILL, 3 * SPILL), 1) - iota((SPILL, 3 * SPILL), 0) - REACH
    pick[...] = jnp.where(turned == -shift, 1.0, 0.0).astype(BF16)
    product[:, 0:LONG] = jnp.zeros((WIDE, LONG), BF16)
    gated[:, 0:REACH] = jnp.zeros((WIDE, REACH), BF16)
    return after - first + shift


def filter_chunk(model, chunk, panels, short_filter, skip, masks, later, taps, circ, direct, query, product, gated):
    row = model * CHUNKS * GROUPS + chunk * GROUPS
    gains = skip[pl.ds(model * CHUNKS + chunk, 1), :]
    direct[...] = jnp.broadcast_to(gains, (WIDE, WIDE)).T
    mask1 = jnp.concatenate([later[...], later[...]], axis=0)

    def short(g, _):
        ch = pl.ds(pl.multiple_of(g * GSIZE, GSIZE), GSIZE)
        line = jnp.broadcast_to(taps[pl.ds(chunk * GROUPS + g, 1), :], (LONG, LONG))
        circ[g] = pltpu.roll(line, 0, 1, stride=1, stride_axis=0).astype(BF16)
        sums = []
        for p in range(3):
            x = panels[p, ch, :].astype(F32)
            f = short_filter[p, pl.ds(row + g, 1), :]
            y = f[:, SHORT - 1 : SHORT] * x
            for j in range(SHORT - 2, -1, -1):
                y = f[:, j : j + 1] * x + mask1 * pltpu.roll(y, 1, 1)
            sums.append(y)
        query[ch, :] = sums[0].astype(BF16)
        product[ch, LONG:] = (sums[1] * sums[2]).astype(BF16)
        return 0

    lax.fori_loop(0, GROUPS, short, 0)

    def long(b, _):
        at = pl.multiple_of(b * LONG, LONG)
        older = masks[b, 0:LONG, :]
        newer = masks[b, LONG : 2 * LONG, :]
        for g in range(GROUPS):
            ch = slice(g * GSIZE, (g + 1) * GSIZE)
            matrix = jnp.concatenate([circ[g] * older, circ[g] * newer], axis=0)
            window = product[ch, pl.ds(at, 2 * LONG)]
            w = jnp.dot(window, matrix, preferred_element_type=F32)
            now = product[ch, pl.ds(at + LONG, LONG)].astype(F32)
            w = w + direct[ch, :] * now
            out = query[ch, pl.ds(at, LONG)].astype(F32) * w
            gated[ch, pl.ds(at + REACH, LONG)] = out.astype(BF16)
        return 0

    lax.fori_loop(0, BLOCKS, long, 0)


def place(limit, k, pick, gated):
    at = k * SPILL
    if not isinstance(k, int):
        at = pl.multiple_of(at, SPILL)
    block = gated[:, pl.ds(at, 3 * SPILL)]
    moved = lax.dot_general(
        pick[...], block, (((1,), (1,)), ((), ())), preferred_element_type=F32
    )
    mine = iota((SPILL, WIDE), 0) + k * SPILL < limit
    return jnp.where(mine, moved, 0.0).astype(BF16)


def filter_kernel(panels, offsets, owners, short_filter, long_filter, skip, out, masks, later, taps, pick, limit, circ, direct, query, product, gated):
    seq = lax.axis_index("seq")
    model = lax.axis_index("mp")
    chunk = pl.program_id(0)

    @pl.when(chunk == 0)
    def _():
        end = prepare(seq, model, offsets, owners, long_filter, masks, later, taps, pick, product, gated)
        limit[...] = jnp.broadcast_to(end, limit.shape)

    filter_chunk(model, chunk, panels, short_filter, skip, masks, later, taps, circ, direct, query, product, gated)
    for k in range(CAP // SPILL):
        out[0, k * SPILL : (k + 1) * SPILL, :] = place(limit[0:1, 0:1], k, pick, gated)


def filter_call(projections, offsets, owners, short_filter, long_filter, skip):
    whole = lambda shape: pl.BlockSpec(shape, lambda i: (0,) * len(shape))
    return pl.pallas_call(
        filter_kernel,
        grid=(CHUNKS,),
        out_shape=jax.ShapeDtypeStruct((CHUNKS, CAP, WIDE), BF16),
        in_specs=[
            pl.BlockSpec((3, WIDE, CAP), lambda i: (0, i, 0)),
            whole(offsets.shape),
            whole(owners.shape),
            whole(short_filter.shape),
            whole(long_filter.shape),
            whole(skip.shape),
        ],
        out_specs=pl.BlockSpec((1, CAP, WIDE), lambda i: (i, 0, 0)),
        scratch_shapes=[
            pltpu.VMEM((BLOCKS, 2 * LONG, LONG), BF16),
            pltpu.VMEM((8, CAP), F32),
            pltpu.VMEM((CHUNKS * GROUPS, LONG), F32),
            pltpu.VMEM((SPILL, 3 * SPILL), BF16),
            pltpu.VMEM((8, 128), jnp.int32),
            pltpu.VMEM((GROUPS, LONG, LONG), BF16),
            pltpu.VMEM((WIDE, WIDE), F32),
            pltpu.VMEM((WIDE, CAP), BF16),
            pltpu.VMEM((WIDE, LONG + CAP), BF16),
            pltpu.VMEM((WIDE, REACH + CAP), BF16),
        ],
    )(projections, offsets, owners, short_filter, long_filter, skip)


N_MP = 8
SIDE = 4
DEPTH = 4 * WIDE
COLS = 1024
ROWS_W = WIDE
HALF = TOK // 2
PIECES = 2 * CHUNKS


def position():
    seq = lax.axis_index("seq")
    return seq, lax.axis_index("mp"), seq // 8, (seq // 2) % SIDE, seq % 2


def seq_at(y, x, core):
    return ((y % SIDE) * SIDE + x % SIDE) * 2 + core


class Links:
    def __init__(self, held, weight, left, right, sems):
        self.held, self.weight, self.left, self.right = held, weight, left, right
        (self.zs, self.zr, self.xs, self.xr, self.ys, self.yr, self.cs, self.cr, self.ss, self.sr) = sems
        self.seq, self.mp, self.y, self.x, self.core = position()

    def enter(self):
        barrier = pltpu.get_barrier_semaphore()
        targets = [{"mp": (self.mp + d) % N_MP} for d in (1, N_MP - 1)]
        targets += [{"seq": (self.seq + d) % 32} for d in (1, 31)]
        targets += [{"seq": seq_at(self.y, self.x + d, self.core)} for d in (1, SIDE - 1)]
        targets += [{"seq": seq_at(self.y + d, self.x, self.core)} for d in (1, SIDE - 1)]
        targets += [{"seq": seq_at(self.y, self.x, 1 - self.core)}]
        for target in targets:
            pl.semaphore_signal(barrier, inc=1, device_id=target, device_id_type=MESH)
        pl.semaphore_wait(barrier, len(targets))

    def z_copy(self, way, step, piece):
        src = (self.mp + (N_MP - step if way == 0 else step)) % N_MP
        ref = self.held.at[src, piece % 2, piece // 2]
        to = (self.mp + (1 if way == 0 else N_MP - 1)) % N_MP
        return pltpu.make_async_remote_copy(
            ref, ref, self.zs.at[way, step, piece], self.zr.at[way, step, piece],
            device_id={"mp": to}, device_id_type=MESH,
        )

    def z_arrived(self, way, step, piece):
        src = (self.mp + (N_MP - step - 1 if way == 0 else step + 1)) % N_MP
        ref = self.held.at[src, piece % 2, piece // 2]
        pltpu.make_async_remote_copy(
            ref, ref, self.zs.at[way, step, piece], self.zr.at[way, step, piece],
            device_id={"mp": self.mp}, device_id_type=MESH,
        ).wait_recv()

    def w_rows(self, y, x, part):
        at = seq_at(y, x, self.core) * ROWS_W
        size = ROWS_W
        if part is not None:
            size = ROWS_W // 2
            at = at + part * size
        return self.weight.at[pl.ds(pl.multiple_of(at, size), size), :]

    def w_copy(self, send, recv, ref, to):
        return pltpu.make_async_remote_copy(
            ref, ref, send, recv, device_id={"seq": to}, device_id_type=MESH
        )

    def x_copy(self, way, step):
        d = 1 if way == 0 else SIDE - 1
        ref = self.w_rows(self.y, self.x + step * (SIDE - d), None if step == 0 else way)
        return self.w_copy(self.xs.at[way, step], self.xr.at[way, step], ref, seq_at(self.y, self.x + d, self.core))

    def x_arrived(self, way, step):
        d = 1 if way == 0 else SIDE - 1
        ref = self.w_rows(self.y, self.x + (step + 1) * (SIDE - d), None if step == 0 else way)
        self.w_copy(self.xs.at[way, step], self.xr.at[way, step], ref, self.seq).wait_recv()

    def y_copy(self, way, step, dx):
        d = 1 if way == 0 else SIDE - 1
        ref = self.w_rows(self.y + step * (SIDE - d), self.x + dx, None if step == 0 else way)
        return self.w_copy(
            self.ys.at[way, step, dx], self.yr.at[way, step, dx], ref, seq_at(self.y + d, self.x, self.core)
        )

    def y_arrived(self, way, step, dx):
        d = 1 if way == 0 else SIDE - 1
        ref = self.w_rows(self.y + (step + 1) * (SIDE - d), self.x + dx, None if step == 0 else way)
        self.w_copy(self.ys.at[way, step, dx], self.yr.at[way, step, dx], ref, self.seq).wait_recv()

    def c_copy(self, dy, dx):
        ref = self.w_rows(self.y + dy, self.x + dx, None)
        return self.w_copy(
            self.cs.at[dy, dx], self.cr.at[dy, dx], ref, seq_at(self.y, self.x, 1 - self.core)
        )

    def c_arrived(self, dy, dx):
        at = seq_at(self.y + dy, self.x + dx, 1 - self.core) * ROWS_W
        ref = self.weight.at[pl.ds(pl.multiple_of(at, ROWS_W), ROWS_W), :]
        self.w_copy(self.cs.at[dy, dx], self.cr.at[dy, dx], ref, self.seq).wait_recv()

    def s_copy(self, way, chunk, ref):
        into = (self.left if way == 0 else self.right).at[chunk]
        to = (self.seq + (1 if way == 0 else 31)) % 32
        return pltpu.make_async_remote_copy(
            ref, into, self.ss.at[way, chunk], self.sr.at[way, chunk],
            device_id={"seq": to}, device_id_type=MESH,
        )

    def w_begin(self):
        for way in (0, 1):
            self.x_copy(way, 0).start()
            self.y_copy(way, 0, 0).start()
        self.c_copy(0, 0).start()

    def w_row(self):
        for way, dx in ((0, SIDE - 1), (1, 1)):
            self.x_arrived(way, 0)
            self.x_copy(way, 1).start()
            for to in (0, 1):
                self.y_copy(to, 0, dx).start()
            self.c_copy(0, dx).start()

    def w_far(self):
        for way in (0, 1):
            self.x_arrived(way, 1)
        for to in (0, 1):
            self.y_copy(to, 0, 2).start()
        self.c_copy(0, 2).start()

    def w_near(self, dx):
        for way, dy in ((0, SIDE - 1), (1, 1)):
            self.y_arrived(way, 0, dx)
            self.y_copy(way, 1, dx).start()
            self.c_copy(dy, dx).start()

    def w_last(self, dx):
        for way in (0, 1):
            self.y_arrived(way, 1, dx)
        self.c_copy(2, dx).start()

    def w_end(self):
        for dy in range(SIDE):
            for dx in range(SIDE):
                self.c_arrived(dy, dx)

    def relay(self, step, piece0, piece1):
        self.z_arrived(0, step - 1, piece0)
        self.z_copy(0, step, piece0).start()
        self.z_arrived(1, step - 1, piece1)
        self.z_copy(1, step, piece1).start()

    def leave(self):
        for way in (0, 1):
            for step in range(2):
                self.x_copy(way, step).wait_send()
                for dx in range(SIDE):
                    self.y_copy(way, step, dx).wait_send()

            def drain(n, _):
                self.z_copy(way, n // PIECES, n % PIECES).wait_send()
                return 0

            lax.fori_loop(0, 3 * PIECES, drain, 0)
            for piece in range(CHUNKS):
                self.z_copy(way, 3, piece + way * CHUNKS).wait_send()
        for dy in range(SIDE):
            for dx in range(SIDE):
                self.c_copy(dy, dx).wait_send()


COLS_STEP = 256


def part_product(held, weight, src, half, chunks, cols):
    lhs = jnp.concatenate([held[src, half, q] for q in chunks], axis=1)
    rhs = jnp.concatenate(
        [weight[pl.ds(pl.multiple_of((src * CHUNKS + q) * WIDE, WIDE), WIDE), cols] for q in chunks], axis=0
    )
    return jnp.dot(lhs, rhs, preferred_element_type=F32)


def columns(n):
    return pl.ds(pl.multiple_of(n * COLS_STEP, COLS_STEP), COLS_STEP)


def add_product(held, weight, total, src, half, chunks):
    def body(n, _):
        cols = columns(n)
        total[half, :, cols] += part_product(held, weight, src, half, chunks, cols)
        return 0

    lax.fori_loop(0, COLS // COLS_STEP, body, 0)


def finish(held, weight, total, staged, src, half, chunks):
    def body(n, _):
        cols = columns(n)
        value = total[half, :, cols] + part_product(held, weight, src, half, chunks, cols)
        staged[half, :, cols] = value.astype(BF16)
        return 0

    lax.fori_loop(0, COLS // COLS_STEP, body, 0)


def source_of(mp, u):
    p = u // 2
    far = (p + 1) // 2
    return (mp + N_MP + far * (1 - 2 * (p % 2))) % N_MP


def add_sources(held, weight, total, mp, low, high):
    def body(u, _):
        add_product(held, weight, total, source_of(mp, u), u % 2, range(CHUNKS))
        return 0

    lax.fori_loop(low, high, body, 0)


def mix_kernel(rows, own_weight, out, held, weight, total, staged, left, right, own_sem, out_sem, *sems):
    links = Links(held, weight, left, right, sems)
    mp = links.mp
    mine = pltpu.make_async_copy(own_weight, links.w_rows(links.y, links.x, None), own_sem)
    mine.start()
    links.enter()
    mine.wait()
    links.w_begin()
    for q in range(CHUNKS):
        links.s_copy(0, q, rows.at[q, CAP - SPILL : CAP]).start()
        links.s_copy(1, q, rows.at[q, 0:SPILL]).start()
    for q in range(CHUNKS):
        held[mp, 0, q] = rows[q, 2 * SPILL : 4 * SPILL]
        for way in (0, 1):
            links.z_copy(way, 0, 2 * q).start()
        for way in (0, 1):
            links.s_copy(way, q, rows.at[q, 0:SPILL]).wait_recv()
        held[mp, 1, q, 0:SPILL] = rows[q, SPILL : 2 * SPILL] + left[q]
        held[mp, 1, q, SPILL : 2 * SPILL] = rows[q, 4 * SPILL : 5 * SPILL] + right[q]
        for way in (0, 1):
            links.z_copy(way, 0, 2 * q + 1).start()
    total[...] = jnp.zeros_like(total)
    links.w_row()
    links.w_far()
    for k in range(PIECES):
        links.relay(1, k, k)
        if k < SIDE:
            links.w_near((0, SIDE - 1, 1, 2)[k])
    for k in range(PIECES):
        links.relay(2, k, k)
        if k < SIDE:
            links.w_last((0, SIDE - 1, 1, 2)[k])
        if k == SIDE:
            links.w_end()
    add_sources(held, weight, total, mp, 0, 6)
    for k in range(CHUNKS):
        links.relay(3, k, k + CHUNKS)
    add_sources(held, weight, total, mp, 6, 10)
    for k in range(CHUNKS):
        links.z_arrived(0, 2, k + CHUNKS)
        links.z_arrived(1, 2, k)
    add_sources(held, weight, total, mp, 10, 14)
    far = (mp + N_MP // 2) % N_MP
    for half in (0, 1):
        links.z_arrived(0, 3, half)
        links.z_arrived(1, 3, half + CHUNKS)
        add_product(held, weight, total, far, half, (0, 2))
    writes = []
    for half in (0, 1):
        links.z_arrived(0, 3, 2 + half)
        links.z_arrived(1, 3, 2 + half + CHUNKS)
        finish(held, weight, total, staged, far, half, (1, 3))
        if half == 0:
            spans = ((0, HALF, SPILL),)
        else:
            spans = ((0, SPILL, 0), (SPILL, HALF, TOK - SPILL))
        for n, (low, high, at) in enumerate(spans):
            copy = pltpu.make_async_copy(
                staged.at[half, low:high], out.at[at : at + high - low], out_sem.at[half, n]
            )
            copy.start()
            writes.append(copy)
    for q in range(CHUNKS):
        links.s_copy(0, q, rows.at[q, CAP - SPILL : CAP]).wait_send()
        links.s_copy(1, q, rows.at[q, 0:SPILL]).wait_send()
    links.leave()
    for copy in writes:
        copy.wait()


LINK_SCRATCH = [
    pltpu.VMEM((N_MP, 2, CHUNKS, HALF, WIDE), BF16),
    pltpu.VMEM((N_MP * DEPTH, COLS), BF16),
    pltpu.VMEM((2, HALF, COLS), F32),
    pltpu.VMEM((2, HALF, COLS), BF16),
    pltpu.VMEM((CHUNKS, SPILL, WIDE), BF16),
    pltpu.VMEM((CHUNKS, SPILL, WIDE), BF16),
    pltpu.SemaphoreType.DMA,
    pltpu.SemaphoreType.DMA((2, 2)),
    pltpu.SemaphoreType.DMA((2, 4, PIECES)),
    pltpu.SemaphoreType.DMA((2, 4, PIECES)),
    pltpu.SemaphoreType.DMA((2, 2)),
    pltpu.SemaphoreType.DMA((2, 2)),
    pltpu.SemaphoreType.DMA((2, 2, SIDE)),
    pltpu.SemaphoreType.DMA((2, 2, SIDE)),
    pltpu.SemaphoreType.DMA((SIDE, SIDE)),
    pltpu.SemaphoreType.DMA((SIDE, SIDE)),
    pltpu.SemaphoreType.DMA((2, CHUNKS)),
    pltpu.SemaphoreType.DMA((2, CHUNKS)),
]


def mix_call(rows, out_weight):
    vmem = pl.BlockSpec(memory_space=pltpu.VMEM)
    anywhere = pl.BlockSpec(memory_space=pl.ANY)
    return pl.pallas_call(
        mix_kernel,
        out_shape=jax.ShapeDtypeStruct((TOK, COLS), BF16),
        in_specs=[vmem, anywhere],
        out_specs=anywhere,
        scratch_shapes=LINK_SCRATCH,
        compiler_params=pltpu.CompilerParams(
            collective_id=0, has_side_effects=True, vmem_limit_bytes=60 * 2**20
        ),
    )(rows, out_weight)


def per_device(projections, lengths, owners, offsets, short_filter, long_filter, skip, out_weight):
    rows = filter_call(
        projections,
        offsets.reshape(1, -1),
        owners.reshape(1, -1),
        short_filter,
        long_filter,
        skip.reshape(-1, WIDE),
    )
    return mix_call(rows, out_weight)


def solution(mesh):
    placed = (P(None, "mp", "seq"), P(), P(), P(), P(), P(), P(), P("seq", "mp"))
    return jax.shard_map(
        per_device, mesh=mesh, in_specs=placed, out_specs=P("seq", "mp"), check_vma=False
    )
```

time: 343 us -> 148 us (0.43)
  the two profiles are of different devices: /device:TPU:1 before, /device:TPU:64 now
where the time goes in v1:
time: 148 us
  Pallas kernels  143 us (97%)
  local copies, waits for them, and re-layouts  4.74 us (3%)
    pallas_call x1, Pallas kernels, mix_call(): pl.pallas_call(mix_kernel, out_shape=jax.ShapeDtypeStruct((TOK, COLS), BF...  101 us
    pallas_call x1, Pallas kernels, filter_call(): pl.pallas_call(filter_kernel, grid=(CHUNKS,), out_shape=jax.ShapeDtypeStr...  41.8 us
    unnamed x2, local copies, waits for them, and re-layouts  4.74 us

profile of v1, /device:TPU:64, one launch (start us, length us, event | category | flops | bytes accessed | tf_op | source)
XLA Modules:
  0.0 147.6 jit_solution(11182575950772992681)
XLA Ops:
  0.0 1.7 %copy.8.short_filter = f32[3,256,7]{2,1,0:T(8,128)} copy(f32[3,256,7]{1,2,0:T(8,128)} %param.11) | data formatting | bytes 43008 | tf_op args[4]
  1.7 41.8 %shard_map.73.rows = bf16[4,1536,128]{2,1,0:T(8,128)(2,1)} custom-call(bf16[3,512,1536]{2,1,0:T(8,128)(2,1)} %panels.1, s32[1,128]{1,0:T(1,128)} %bitcast.4, s32[1,128]{1,0:T(1,128)} %bitcast.5, f32[3,256,7]{2,1,0:T(8,128)} %copy.8.short_filter, bf16[256,128]{1,0:T(8,128)(2,1)} %long_filter.1, f32[32,128]{1,0:T(8,128)} %bitcast.3), custom_call_target="tpu_custom_call" | custom-call | tf_op jit(solution)/shard_map/pallas_call | solution.py:133
  43.5 101.0 %shard_map.74 = bf16[1024,1024]{1,0:T(8,128)(2,1)} custom-call(bf16[4,1536,128]{2,1,0:T(8,128)(2,1)} %shard_map.73.rows, bf16[128,1024]{1,0:T(8,128)(2,1)} %own_weight.1), custom_call_target="tpu_custom_call" | custom-call | tf_op jit(solution)/shard_map/pallas_call | solution.py:472
  144.5 3.1 %copy.10 = bf16[1024,1024]{1,0:T(8,128)(2,1)} copy(bf16[1024,1024]{1,0:T(8,128)(2,1)} %shard_map.74) | data formatting | bytes 4194304

commit v2 on v1

--- a/solution.py
+++ b/solution.py
@@ -29,7 +29,7 @@
     return lax.broadcasted_iota(jnp.int32, shape, dim)
 
 
-def prepare(seq, model, offsets, owners, long_filter, masks, later, taps, pick, product, gated):
+def prepare(seq, model, offsets, owners, short_filter, long_filter, masks, later, near, taps, pick, product, gated):
     off = offsets[...]
     own = owners[...]
     first = jnp.min(jnp.where(own == seq, off, TOKENS), axis=1, keepdims=True)
@@ -46,11 +46,16 @@
         newer = (lag >= 0) & (lag <= pos)
         masks[b, 0:LONG, :] = jnp.where(older, 1.0, 0.0).astype(BF16)
         masks[b, LONG : 2 * LONG, :] = jnp.where(newer, 1.0, 0.0).astype(BF16)
-        later[:, b * LONG : (b + 1) * LONG] = jnp.broadcast_to(
-            jnp.where(pos >= 1, 1.0, 0.0), (8, LONG)
-        )
+        for j in range(1, SHORT):
+            later[j - 1, :, b * LONG : (b + 1) * LONG] = jnp.broadcast_to(
+                jnp.where(pos >= j, 1.0, 0.0), (8, LONG)
+            )
     rows = CHUNKS * GROUPS
     taps[...] = long_filter[pl.ds(pl.multiple_of(model * rows, rows), rows), :].astype(F32)
+    aside = pl.ds(pl.multiple_of(model // 4 * WIDE, WIDE), WIDE)
+    for p in range(3):
+        block = jnp.concatenate([short_filter[p, :, aside], jnp.zeros((WIDE - SHORT, WIDE), F32)], axis=0)
+        near[p] = block.T
     shift = first - seq * TOK + SPILL
     turned = iota((SPILL, 3 * SPILL), 1) - iota((SPILL, 3 * SPILL), 0) - REACH
     pick[...] = jnp.where(turned == -shift, 1.0, 0.0).astype(BF16)
@@ -59,30 +64,48 @@
     return after - first + shift
 
 
-def filter_chunk(model, chunk, panels, short_filter, skip, masks, later, taps, circ, direct, query, product, gated):
-    row = model * CHUNKS * GROUPS + chunk * GROUPS
+def short_stage(model, chunk, panels, near, skip, later, taps, circ, direct, query, product):
+    row = model % 4 * (CHUNKS * GROUPS) + chunk * GROUPS
     gains = skip[pl.ds(model * CHUNKS + chunk, 1), :]
     direct[...] = jnp.broadcast_to(gains, (WIDE, WIDE)).T
-    mask1 = jnp.concatenate([later[...], later[...]], axis=0)
+    lane = iota((GSIZE, LONG), 1)
 
     def short(g, _):
         ch = pl.ds(pl.multiple_of(g * GSIZE, GSIZE), GSIZE)
         line = jnp.broadcast_to(taps[pl.ds(chunk * GROUPS + g, 1), :], (LONG, LONG))
         circ[g] = pltpu.roll(line, 0, 1, stride=1, stride_axis=0).astype(BF16)
-        sums = []
+        factor = []
         for p in range(3):
-            x = panels[p, ch, :].astype(F32)
-            f = short_filter[p, pl.ds(row + g, 1), :]
-            y = f[:, SHORT - 1 : SHORT] * x
-            for j in range(SHORT - 2, -1, -1):
-                y = f[:, j : j + 1] * x + mask1 * pltpu.roll(y, 1, 1)
-            sums.append(y)
-        query[ch, :] = sums[0].astype(BF16)
-        product[ch, LONG:] = (sums[1] * sums[2]).astype(BF16)
+            f = near[p, pl.ds(row + g, 1), :]
+            factor.append([jnp.broadcast_to(f[:, j : j + 1], (8, LONG)) for j in range(SHORT)])
+        rolled = [[None] * SHORT for _ in range(3)]
+        for b in range(BLOCKS):
+            at = slice(b * LONG, (b + 1) * LONG)
+            sums = []
+            for p in range(3):
+                x = panels[chunk, p, ch, at]
+                wide = x.astype(F32)
+                low = factor[p][0] * wide[0:8]
+                high = factor[p][0] * wide[8:16]
+                for j in range(1, SHORT):
+                    turned = pltpu.roll(x, j, 1)
+                    before = rolled[p][j]
+                    rolled[p][j] = turned
+                    if b > 0:
+                        turned = jnp.where(lane < j, before, turned)
+                    weight = factor[p][j] * later[j - 1, :, at]
+                    wide = turned.astype(F32)
+                    low = low + weight * wide[0:8]
+                    high = high + weight * wide[8:16]
+                sums.append(jnp.concatenate([low, high], axis=0))
+            query[ch, at] = sums[0].astype(BF16)
+            product[ch, (b + 1) * LONG : (b + 2) * LONG] = (sums[1] * sums[2]).astype(BF16)
         return 0
 
     lax.fori_loop(0, GROUPS, short, 0)
 
+
+def long_stage(masks, circ, direct, query, product, gated):
     def long(b, _):
         at = pl.multiple_of(b * LONG, LONG)
         older = masks[b, 0:LONG, :]
@@ -113,51 +136,6 @@
     return jnp.where(mine, moved, 0.0).astype(BF16)
 
 
-def filter_kernel(panels, offsets, owners, short_filter, long_filter, skip, out, masks, later, taps, pick, limit, circ, direct, query, product, gated):
-    seq = lax.axis_index("seq")
-    model = lax.axis_index("mp")
-    chunk = pl.program_id(0)
-
-    @pl.when(chunk == 0)
-    def _():
-        end = prepare(seq, model, offsets, owners, long_filter, masks, later, taps, pick, product, gated)
-        limit[...] = jnp.broadcast_to(end, limit.shape)
-
-    filter_chunk(model, chunk, panels, short_filter, skip, masks, later, taps, circ, direct, query, product, gated)
-    for k in range(CAP // SPILL):
-        out[0, k * SPILL : (k + 1) * SPILL, :] = place(limit[0:1, 0:1], k, pick, gated)
-
-
-def filter_call(projections, offsets, owners, short_filter, long_filter, skip):
-    whole = lambda shape: pl.BlockSpec(shape, lambda i: (0,) * len(shape))
-    return pl.pallas_call(
-        filter_kernel,
-        grid=(CHUNKS,),
-        out_shape=jax.ShapeDtypeStruct((CHUNKS, CAP, WIDE), BF16),
-        in_specs=[
-            pl.BlockSpec((3, WIDE, CAP), lambda i: (0, i, 0)),
-            whole(offsets.shape),
-            whole(owners.shape),
-            whole(short_filter.shape),
-            whole(long_filter.shape),
-            whole(skip.shape),
-        ],
-        out_specs=pl.BlockSpec((1, CAP, WIDE), lambda i: (i, 0, 0)),
-        scratch_shapes=[
-            pltpu.VMEM((BLOCKS, 2 * LONG, LONG), BF16),
-            pltpu.VMEM((8, CAP), F32),
-            pltpu.VMEM((CHUNKS * GROUPS, LONG), F32),
-            pltpu.VMEM((SPILL, 3 * SPILL), BF16),
-            pltpu.VMEM((8, 128), jnp.int32),
-            pltpu.VMEM((GROUPS, LONG, LONG), BF16),
-            pltpu.VMEM((WIDE, WIDE), F32),
-            pltpu.VMEM((WIDE, CAP), BF16),
-            pltpu.VMEM((WIDE, LONG + CAP), BF16),
-            pltpu.VMEM((WIDE, REACH + CAP), BF16),
-        ],
-    )(projections, offsets, owners, short_filter, long_filter, skip)
-
-
 N_MP = 8
 SIDE = 4
 DEPTH = 4 * WIDE
@@ -182,7 +160,7 @@
         (self.zs, self.zr, self.xs, self.xr, self.ys, self.yr, self.cs, self.cr, self.ss, self.sr) = sems
         self.seq, self.mp, self.y, self.x, self.core = position()
 
-    def enter(self):
+    def greet(self):
         barrier = pltpu.get_barrier_semaphore()
         targets = [{"mp": (self.mp + d) % N_MP} for d in (1, N_MP - 1)]
         targets += [{"seq": (self.seq + d) % 32} for d in (1, 31)]
@@ -191,7 +169,9 @@
         targets += [{"seq": seq_at(self.y, self.x, 1 - self.core)}]
         for target in targets:
             pl.semaphore_signal(barrier, inc=1, device_id=target, device_id_type=MESH)
-        pl.semaphore_wait(barrier, len(targets))
+
+    def meet(self):
+        pl.semaphore_wait(pltpu.get_barrier_semaphore(), 9)
 
     def z_copy(self, way, step, piece):
         src = (self.mp + (N_MP - step if way == 0 else step)) % N_MP
@@ -374,34 +354,78 @@
     lax.fori_loop(low, high, body, 0)
 
 
-def mix_kernel(rows, own_weight, out, held, weight, total, staged, left, right, own_sem, out_sem, *sems):
-    links = Links(held, weight, left, right, sems)
+def mix_kernel(projections, own_weight, offsets, owners, short_filter, long_filter, skip, out, *scratch):
+    panels, masks, later, near, taps, pick, circ, direct, query, product, gated = scratch[:11]
+    mine, outgoing, held, weight, total, staged, left, right, in_sem, own_sem, out_sem = scratch[11:22]
+    links = Links(held, weight, left, right, scratch[22:])
     mp = links.mp
-    mine = pltpu.make_async_copy(own_weight, links.w_rows(links.y, links.x, None), own_sem)
-    mine.start()
-    links.enter()
-    mine.wait()
+
+    def fetch(q):
+        return pltpu.make_async_copy(
+            projections.at[:, pl.ds(pl.multiple_of(q * WIDE, WIDE), WIDE), :], panels.at[q], in_sem.at[q]
+        )
+
+    own = pltpu.make_async_copy(own_weight, links.w_rows(links.y, links.x, None), own_sem)
+    own.start()
+    for q in range(CHUNKS):
+        fetch(q).start()
+    links.greet()
+    limit = prepare(
+        links.seq, mp, offsets, owners, short_filter, long_filter, masks, later, near, taps, pick, product, gated
+    )
+    total[...] = jnp.zeros_like(total)
+    links.meet()
+    own.wait()
     links.w_begin()
-    for q in range(CHUNKS):
-        links.s_copy(0, q, rows.at[q, CAP - SPILL : CAP]).start()
-        links.s_copy(1, q, rows.at[q, 0:SPILL]).start()
-    for q in range(CHUNKS):
-        held[mp, 0, q] = rows[q, 2 * SPILL : 4 * SPILL]
+
+    def spill(way, q):
+        return links.s_copy(way, q, outgoing.at[q, way])
+
+    def edges(q):
+        for way in (0, 1):
+            spill(way, q).wait_recv()
+        held[mp, 1, q, 0:SPILL] = mine[0] + left[q]
+        held[mp, 1, q, SPILL : 2 * SPILL] = mine[1] + right[q]
+        for way in (0, 1):
+            links.z_copy(way, 0, 2 * q + 1).start()
+
+    def chunk(q, _):
+        fetch(q).wait()
+        short_stage(mp, q, panels, near, skip, later, taps, circ, direct, query, product)
+
+        @pl.when(q >= 1)
+        def _():
+            edges(q - 1)
+            links.relay(1, 2 * q - 2, 2 * q - 2)
+
+        for n, step in ((1, links.w_row), (2, lambda: links.w_near(0)), (3, lambda: links.w_near(1))):
+            pl.when(q == n)(step)
+        long_stage(masks, circ, direct, query, product, gated)
+        outgoing[q, 0] = place(limit, 5, pick, gated)
+        outgoing[q, 1] = place(limit, 0, pick, gated)
+        for way in (0, 1):
+            spill(way, q).start()
+        held[mp, 0, q, 0:SPILL] = place(limit, 2, pick, gated)
+        held[mp, 0, q, SPILL : 2 * SPILL] = place(limit, 3, pick, gated)
         for way in (0, 1):
             links.z_copy(way, 0, 2 * q).start()
-        for way in (0, 1):
-            links.s_copy(way, q, rows.at[q, 0:SPILL]).wait_recv()
-        held[mp, 1, q, 0:SPILL] = rows[q, SPILL : 2 * SPILL] + left[q]
-        held[mp, 1, q, SPILL : 2 * SPILL] = rows[q, 4 * SPILL : 5 * SPILL] + right[q]
-        for way in (0, 1):
-            links.z_copy(way, 0, 2 * q + 1).start()
-    total[...] = jnp.zeros_like(total)
-    links.w_row()
-    links.w_far()
-    for k in range(PIECES):
+        mine[0] = place(limit, 1, pick, gated)
+        mine[1] = place(limit, 4, pick, gated)
+
+        @pl.when(q >= 1)
+        def _():
+            links.relay(1, 2 * q - 1, 2 * q - 1)
+
+        for n, step in (
+            (1, links.w_far), (2, lambda: links.w_near(SIDE - 1)), (3, lambda: links.w_near(2))
+        ):
+            pl.when(q == n)(step)
+        return 0
+
+    lax.fori_loop(0, CHUNKS, chunk, 0)
+    edges(CHUNKS - 1)
+    for k in (PIECES - 2, PIECES - 1):
         links.relay(1, k, k)
-        if k < SIDE:
-            links.w_near((0, SIDE - 1, 1, 2)[k])
     for k in range(PIECES):
         links.relay(2, k, k)
         if k < SIDE:
@@ -437,13 +461,28 @@
             copy.start()
             writes.append(copy)
     for q in range(CHUNKS):
-        links.s_copy(0, q, rows.at[q, CAP - SPILL : CAP]).wait_send()
-        links.s_copy(1, q, rows.at[q, 0:SPILL]).wait_send()
+        for way in (0, 1):
+            spill(way, q).wait_send()
     links.leave()
     for copy in writes:
         copy.wait()
 
 
+FILTER_SCRATCH = [
+    pltpu.VMEM((CHUNKS, 3, WIDE, CAP), BF16),
+    pltpu.VMEM((BLOCKS, 2 * LONG, LONG), BF16),
+    pltpu.VMEM((SHORT - 1, 8, CAP), F32),
+    pltpu.VMEM((3, WIDE, WIDE), F32),
+    pltpu.VMEM((CHUNKS * GROUPS, LONG), F32),
+    pltpu.VMEM((SPILL, 3 * SPILL), BF16),
+    pltpu.VMEM((GROUPS, LONG, LONG), BF16),
+    pltpu.VMEM((WIDE, WIDE), F32),
+    pltpu.VMEM((WIDE, CAP), BF16),
+    pltpu.VMEM((WIDE, LONG + CAP), BF16),
+    pltpu.VMEM((WIDE, REACH + CAP), BF16),
+    pltpu.VMEM((2, SPILL, WIDE), BF16),
+    pltpu.VMEM((CHUNKS, 2, SPILL, WIDE), BF16),
+]
 LINK_SCRATCH = [
     pltpu.VMEM((N_MP, 2, CHUNKS, HALF, WIDE), BF16),
     pltpu.VMEM((N_MP * DEPTH, COLS), BF16),
@@ -451,6 +490,7 @@
     pltpu.VMEM((2, HALF, COLS), BF16),
     pltpu.VMEM((CHUNKS, SPILL, WIDE), BF16),
     pltpu.VMEM((CHUNKS, SPILL, WIDE), BF16),
+    pltpu.SemaphoreType.DMA((CHUNKS,)),
     pltpu.SemaphoreType.DMA,
     pltpu.SemaphoreType.DMA((2, 2)),
     pltpu.SemaphoreType.DMA((2, 4, PIECES)),
@@ -466,31 +506,27 @@
 ]
 
 
-def mix_call(rows, out_weight):
+def per_device(projections, lengths, owners, offsets, short_filter, long_filter, skip, out_weight):
     vmem = pl.BlockSpec(memory_space=pltpu.VMEM)
     anywhere = pl.BlockSpec(memory_space=pl.ANY)
     return pl.pallas_call(
         mix_kernel,
         out_shape=jax.ShapeDtypeStruct((TOK, COLS), BF16),
-        in_specs=[vmem, anywhere],
+        in_specs=[anywhere, anywhere] + [vmem] * 5,
         out_specs=anywhere,
-        scratch_shapes=LINK_SCRATCH,
+        scratch_shapes=FILTER_SCRATCH + LINK_SCRATCH,
         compiler_params=pltpu.CompilerParams(
             collective_id=0, has_side_effects=True, vmem_limit_bytes=60 * 2**20
         ),
-    )(rows, out_weight)
-
-
-def per_device(projections, lengths, owners, offsets, short_filter, long_filter, skip, out_weight):
-    rows = filter_call(
+    )(
         projections,
+        out_weight,
         offsets.reshape(1, -1),
         owners.reshape(1, -1),
-        short_filter,
+        short_filter.transpose(0, 2, 1),
         long_filter,
         skip.reshape(-1, WIDE),
     )
-    return mix_call(rows, out_weight)
 
 
 def solution(mesh):

time: 148 us -> 106 us (0.72)
  Pallas kernels: 143 us -> 102 us
  local copies, waits for them, and re-layouts: 4.74 us -> 3.08 us
    pallas_call x2 -> x1, Pallas kernels: 143 us -> 102 us  [per_device(): pl.pallas_call(mix_kernel, out_shape=jax.ShapeDtypeStruct((TOK, COLS), BF...]
    unnamed x2 -> x1, local copies, waits for them, and re-layouts: 4.74 us -> 3.08 us
where the time goes in v2:
time: 106 us
  Pallas kernels  102 us (96%)
  local copies, waits for them, and re-layouts  3.08 us (3%)
    pallas_call x1, Pallas kernels, per_device(): pl.pallas_call(mix_kernel, out_shape=jax.ShapeDtypeStruct((TOK, COLS), BF...  102 us
    unnamed x1, local copies, waits for them, and re-layouts  3.08 us

profile of v2, /device:TPU:64, one launch (start us, length us, event | category | flops | bytes accessed | tf_op | source)
XLA Modules:
  0.0 105.6 jit_solution(9662538281498926737)
XLA Ops:
  0.0 102.5 %shard_map.73 = bf16[1024,1024]{1,0:T(8,128)(2,1)} custom-call(bf16[3,512,1536]{2,1,0:T(8,128)(2,1)} %projections.1, bf16[128,1024]{1,0:T(8,128)(2,1)} %own_weight.1, s32[1,128]{1,0:T(1,128)} %bitcast.6, s32[1,128]{1,0:T(1,128)} %bitcast.7, f32[3,7,256]{2,1,0:T(8,128)} %bitcast.4, bf16[256,128]{1,0:T(8,128)(2,1)} %long_filter.1, f32[32,128]{1,0:T(8,128)} %bitcast.5), custom_call_target="tpu_custom_call" | custom-call | tf_op jit(solution)/shard_map/pallas_call | solution.py:512
  102.5 3.1 %copy.9 = bf16[1024,1024]{1,0:T(8,128)(2,1)} copy(bf16[1024,1024]{1,0:T(8,128)(2,1)} %shard_map.73) | data formatting | bytes 4194304

commit v3 on v2

v3 whole, which is shorter than its diff:
```python
import functools

import jax
import jax.numpy as jnp
from jax import lax
from jax.experimental import pallas as pl
from jax.experimental.pallas import tpu as pltpu
from jax.sharding import PartitionSpec as P

MESH = pl.DeviceIdType.MESH
F32 = jnp.float32
BF16 = jnp.bfloat16

GSIZE = 16
SHORT = 7
LONG = 128
TOK = 1024
SPILL = 256
CAP = 1536
TOKENS = 32768
WIDE = 128
CHUNKS = 4
GROUPS = WIDE // GSIZE
BLOCKS = CAP // LONG
REACH = 2 * SPILL


def iota(shape, dim):
    return lax.broadcasted_iota(jnp.int32, shape, dim)


def prepare(seq, model, offsets, owners, short_filter, long_filter, masks, later, near, taps, pick, product, gated):
    off = offsets[...]
    own = owners[...]
    first = jnp.min(jnp.where(own == seq, off, TOKENS), axis=1, keepdims=True)
    after = jnp.min(jnp.where(own == seq + 1, off, TOKENS), axis=1, keepdims=True)
    shift = first - seq * TOK + SPILL
    column = jnp.broadcast_to(off, (LONG, LONG)).T
    lag = iota((LONG, LONG), 1) - iota((LONG, LONG), 0)
    older = jnp.where(lag < 0, lag + LONG, TOKENS)
    newer = jnp.where(lag >= 0, lag, TOKENS)
    for b in range(BLOCKS):
        token = first + iota((1, LONG), 1) + b * LONG
        begin = jnp.max(jnp.where(column <= token, column, 0), axis=0, keepdims=True)
        pos = jnp.broadcast_to(token - begin, (8, LONG))
        wide = jnp.broadcast_to(token - begin, (LONG, LONG))
        masks[b, 0:LONG, :] = jnp.where(older <= wide, 1.0, 0.0).astype(BF16)
        masks[b, LONG : 2 * LONG, :] = jnp.where(newer <= wide, 1.0, 0.0).astype(BF16)
        for j in range(1, SHORT):
            later[j - 1, :, b * LONG : (b + 1) * LONG] = jnp.where(pos >= j, 1.0, 0.0)
    rows = CHUNKS * GROUPS
    taps[...] = long_filter[pl.ds(pl.multiple_of(model * rows, rows), rows), :].astype(F32)
    aside = pl.ds(pl.multiple_of(model // 4 * WIDE, WIDE), WIDE)
    for p in range(3):
        block = jnp.concatenate([short_filter[p, :, aside], jnp.zeros((WIDE - SHORT, WIDE), F32)], axis=0)
        near[p] = block.T
    turned = iota((SPILL, 3 * SPILL), 1) - iota((SPILL, 3 * SPILL), 0) - REACH
    pick[...] = jnp.where(turned == -shift, 1.0, 0.0).astype(BF16)
    product[:, 0:LONG] = jnp.zeros((WIDE, LONG), BF16)
    gated[:, 0:REACH] = jnp.zeros((WIDE, REACH), BF16)
    return after - first + shift


def short_stage(model, chunk, low_block, high_block, panels, near, skip, later, taps, circ, direct, query, product):
    row = model % 4 * (CHUNKS * GROUPS) + chunk * GROUPS
    if low_block == 0:
        gains = skip[pl.ds(model * CHUNKS + chunk, 1), :]
        direct[...] = jnp.broadcast_to(gains, (WIDE, WIDE)).T
    lane = iota((GSIZE, LONG), 1)

    def short(g, _):
        ch = pl.ds(pl.multiple_of(g * GSIZE, GSIZE), GSIZE)
        if low_block == 0:
            line = jnp.broadcast_to(taps[pl.ds(chunk * GROUPS + g, 1), :], (LONG, LONG))
            circ[g] = pltpu.roll(line, 0, 1, stride=1, stride_axis=0).astype(BF16)
        factor = []
        for p in range(3):
            f = near[p, pl.ds(row + g, 1), :]
            factor.append([jnp.broadcast_to(f[:, j : j + 1], (8, LONG)) for j in range(SHORT)])
        rolled = [[None] * SHORT for _ in range(3)]
        if low_block > 0:
            at = slice((low_block - 1) * LONG, low_block * LONG)
            rolled = [[pltpu.roll(panels[chunk, p, ch, at], j, 1) for j in range(SHORT)] for p in range(3)]
        for b in range(low_block, high_block):
            at = slice(b * LONG, (b + 1) * LONG)
            sums = []
            for p in range(3):
                x = panels[chunk, p, ch, at]
                wide = x.astype(F32)
                low = factor[p][0] * wide[0:8]
                high = factor[p][0] * wide[8:16]
                for j in range(1, SHORT):
                    turned = pltpu.roll(x, j, 1)
                    before = rolled[p][j]
                    rolled[p][j] = turned
                    if b > 0:
                        turned = jnp.where(lane < j, before, turned)
                    weight = factor[p][j] * later[j - 1, :, at]
                    wide = turned.astype(F32)
                    low = low + weight * wide[0:8]
                    high = high + weight * wide[8:16]
                sums.append(jnp.concatenate([low, high], axis=0))
            query[ch, at] = sums[0].astype(BF16)
            product[ch, (b + 1) * LONG : (b + 2) * LONG] = (sums[1] * sums[2]).astype(BF16)
        return 0

    lax.fori_loop(0, GROUPS, short, 0)


def long_stage(low_block, high_block, masks, circ, direct, query, product, gated):
    def long(b, _):
        at = pl.multiple_of(b * LONG, LONG)
        older = masks[b, 0:LONG, :]
        newer = masks[b, LONG : 2 * LONG, :]
        for g in range(GROUPS):
            ch = slice(g * GSIZE, (g + 1) * GSIZE)
            matrix = jnp.concatenate([circ[g] * older, circ[g] * newer], axis=0)
            window = product[ch, pl.ds(at, 2 * LONG)]
            w = jnp.dot(window, matrix, preferred_element_type=F32)
            now = product[ch, pl.ds(at + LONG, LONG)].astype(F32)
            w = w + direct[ch, :] * now
            out = query[ch, pl.ds(at, LONG)].astype(F32) * w
            gated[ch, pl.ds(at + REACH, LONG)] = out.astype(BF16)
        return 0

    lax.fori_loop(low_block, high_block, long, 0)


def place(limit, k, pick, gated):
    at = k * SPILL
    if not isinstance(k, int):
        at = pl.multiple_of(at, SPILL)
    block = gated[:, pl.ds(at, 3 * SPILL)]
    moved = lax.dot_general(
        pick[...], block, (((1,), (1,)), ((), ())), preferred_element_type=F32
    )
    mine = iota((SPILL, WIDE), 0) + k * SPILL < limit
    return jnp.where(mine, moved, 0.0).astype(BF16)


N_MP = 8
SIDE = 4
DEPTH = 4 * WIDE
COLS = 1024
ROWS_W = WIDE
HALF = TOK // 2
PIECES = 2 * CHUNKS


def position():
    seq = lax.axis_index("seq")
    return seq, lax.axis_index("mp"), seq // 8, (seq // 2) % SIDE, seq % 2


def seq_at(y, x, core):
    return ((y % SIDE) * SIDE + x % SIDE) * 2 + core


class Links:
    def __init__(self, held, weight, left, right, sems):
        self.held, self.weight, self.left, self.right = held, weight, left, right
        (self.zs, self.zf, self.zr, self.ws, self.xr, self.yr, self.cr, self.ss, self.sr) = sems
        self.seq, self.mp, self.y, self.x, self.core = position()

    def greet(self):
        barrier = pltpu.get_barrier_semaphore()
        targets = [{"mp": (self.mp + d) % N_MP} for d in (1, N_MP - 1)]
        targets += [{"seq": (self.seq + d) % 32} for d in (1, 31)]
        targets += [{"seq": seq_at(self.y, self.x + d, self.core)} for d in (1, SIDE - 1)]
        targets += [{"seq": seq_at(self.y + d, self.x, self.core)} for d in (1, SIDE - 1)]
        targets += [{"seq": seq_at(self.y, self.x, 1 - self.core)}]
        for target in targets:
            pl.semaphore_signal(barrier, inc=1, device_id=target, device_id_type=MESH)

    def meet(self):
        pl.semaphore_wait(pltpu.get_barrier_semaphore(), 9)

    def z_push(self, way, ref, recv, late=0):
        to = (self.mp + (1 if way == 0 else N_MP - 1)) % N_MP
        pltpu.make_async_remote_copy(
            ref, ref, self.zs.at[way, late], recv, device_id={"mp": to}, device_id_type=MESH
        ).start()

    def z_take(self, ref, recv):
        pltpu.make_async_copy(ref, ref, recv).wait()

    def own_part(self, src, chunk, part):
        if part == 2:
            return self.held.at[src, 1, chunk]
        return self.held.at[src, 0, chunk, part * SPILL : (part + 1) * SPILL]

    def z_begin(self, chunk, part):
        for way in (0, 1):
            self.z_push(way, self.own_part(self.mp, chunk, part), self.zf.at[way, chunk, part])

    def behind(self, way, step):
        return (self.mp + (N_MP - step if way == 0 else step)) % N_MP

    def z_first(self, chunk, parts):
        for way in (0, 1):
            src = self.behind(way, 1)
            for part in parts:
                self.z_take(self.own_part(src, chunk, part), self.zf.at[way, chunk, part])
            half = parts[-1] // 2
            self.z_push(way, self.held.at[src, half, chunk], self.zr.at[way, 0, 2 * chunk + half])

    def z_ref(self, way, step, piece):
        return self.held.at[self.behind(way, step + 1), piece % 2, piece // 2]

    def z_arrived(self, way, step, piece):
        self.z_take(self.z_ref(way, step, piece), self.zr.at[way, step - 1, piece])

    def relay(self, way, step, pieces):
        late = 1 if step == 3 else 0
        for piece in pieces:
            self.z_arrived(way, step - 1, piece)
            self.z_push(way, self.z_ref(way, step - 1, piece), self.zr.at[way, step - 1, piece], late)

    def w_rows(self, y, x, part):
        at = seq_at(y, x, self.core) * ROWS_W
        size = ROWS_W
        if part is not None:
            size = ROWS_W // 2
            at = at + part * size
        return self.weight.at[pl.ds(pl.multiple_of(at, size), size), :]

    def w_copy(self, send, recv, ref, to):
        return pltpu.make_async_remote_copy(
            ref, ref, send, recv, device_id={"seq": to}, device_id_type=MESH
        )

    def x_copy(self, way, step):
        d = 1 if way == 0 else SIDE - 1
        ref = self.w_rows(self.y, self.x + step * (SIDE - d), None if step == 0 else way)
        return self.w_copy(self.ws, self.xr.at[way, step], ref, seq_at(self.y, self.x + d, self.core))

    def x_arrived(self, way, step):
        d = 1 if way == 0 else SIDE - 1
        ref = self.w_rows(self.y, self.x + (step + 1) * (SIDE - d), None if step == 0 else way)
        self.z_take(ref, self.xr.at[way, step])

    def y_copy(self, way, step, dx):
        d = 1 if way == 0 else SIDE - 1
        ref = self.w_rows(self.y + step * (SIDE - d), self.x + dx, None if step == 0 else way)
        return self.w_copy(
            self.ws, self.yr.at[way, step, dx], ref, seq_at(self.y + d, self.x, self.core)
        )

    def y_arrived(self, way, step, dx):
        d = 1 if way == 0 else SIDE - 1
        ref = self.w_rows(self.y + (step + 1) * (SIDE - d), self.x + dx, None if step == 0 else way)
        self.z_take(ref, self.yr.at[way, step, dx])

    def c_copy(self, dy, dx):
        ref = self.w_rows(self.y + dy, self.x + dx, None)
        return self.w_copy(
            self.ws, self.cr.at[dy, dx], ref, seq_at(self.y, self.x, 1 - self.core)
        )

    def c_arrived(self, dy, dx):
        at = seq_at(self.y + dy, self.x + dx, 1 - self.core) * ROWS_W
        ref = self.weight.at[pl.ds(pl.multiple_of(at, ROWS_W), ROWS_W), :]
        self.z_take(ref, self.cr.at[dy, dx])

    def s_copy(self, way, chunk, ref):
        into = (self.left if way == 0 else self.right).at[chunk]
        to = (self.seq + (1 if way == 0 else 31)) % 32
        return pltpu.make_async_remote_copy(
            ref, into, self.ss, self.sr.at[way, chunk],
            device_id={"seq": to}, device_id_type=MESH,
        )

    def w_begin(self):
        for way in (0, 1):
            self.x_copy(way, 0).start()
            self.y_copy(way, 0, 0).start()
        self.c_copy(0, 0).start()

    def w_row(self):
        for way, dx in ((0, SIDE - 1), (1, 1)):
            self.x_arrived(way, 0)
            self.x_copy(way, 1).start()
            for to in (0, 1):
                self.y_copy(to, 0, dx).start()
            self.c_copy(0, dx).start()

    def w_far(self):
        for way in (0, 1):
            self.x_arrived(way, 1)
        for to in (0, 1):
            self.y_copy(to, 0, 2).start()
        self.c_copy(0, 2).start()

    def w_near(self, dx):
        for way, dy in ((0, SIDE - 1), (1, 1)):
            self.y_arrived(way, 0, dx)
            self.y_copy(way, 1, dx).start()
            self.c_copy(dy, dx).start()

    def w_last(self, dx):
        for way in (0, 1):
            self.y_arrived(way, 1, dx)
        self.c_copy(2, dx).start()

    def w_end(self):
        for dy in range(SIDE):
            for dx in range(SIDE):
                self.c_arrived(dy, dx)

    def leave(self):
        for way in (0, 1):
            ref = self.held.at[0 : N_MP // 2 - 1]
            self.z_take(ref, self.zs.at[way, 0])
            self.z_take(self.held.at[0, 0], self.zs.at[way, 1])
        sent = (2 + 2 * SIDE) * (ROWS_W + ROWS_W // 2) + SIDE * SIDE * ROWS_W
        self.z_take(self.weight.at[0:sent], self.ws)
        self.z_take(self.held.at[0, 0], self.ss)


COLS_STEP = 256


def part_product(held, weight, src, half, chunks, cols):
    lhs = jnp.concatenate([held[src, half, q] for q in chunks], axis=1)
    rhs = jnp.concatenate(
        [weight[pl.ds(pl.multiple_of((src * CHUNKS + q) * WIDE, WIDE), WIDE), cols] for q in chunks], axis=0
    )
    return jnp.dot(lhs, rhs, preferred_element_type=F32)


def columns(n):
    return pl.ds(pl.multiple_of(n * COLS_STEP, COLS_STEP), COLS_STEP)


def add_product(held, weight, total, src, half, chunks, fresh=False):
    def body(n, _):
        cols = columns(n)
        value = part_product(held, weight, src, half, chunks, cols)
        if fresh:
            total[half, :, cols] = value
        else:
            total[half, :, cols] += value
        return 0

    lax.fori_loop(0, COLS // COLS_STEP, body, 0)


def finish(held, weight, total, out, src, half, chunks):
    def body(n, _):
        cols = columns(n)
        value = (total[half, :, cols] + part_product(held, weight, src, half, chunks, cols)).astype(BF16)
        if half == 0:
            out[SPILL : SPILL + HALF, cols] = value
        else:
            out[0:SPILL, cols] = value[0:SPILL]
            out[TOK - SPILL : TOK, cols] = value[SPILL:]
        return 0

    lax.fori_loop(0, COLS // COLS_STEP, body, 0)


def source_of(mp, u):
    p = u // 2
    far = (p + 1) // 2
    return (mp + N_MP + far * (1 - 2 * (p % 2))) % N_MP


def add_sources(held, weight, total, mp, low, high):
    def body(u, _):
        add_product(held, weight, total, source_of(mp, u), u % 2, range(CHUNKS))
        return 0

    lax.fori_loop(low, high, body, 0)


SEGMENTS = ((0, 6), (6, 8), (8, BLOCKS))


def mix_kernel(projections, own_weight, offsets, owners, short_filter, long_filter, skip, out, *scratch):
    panels, masks, later, near, taps, pick, circ, direct, query, product, gated = scratch[:11]
    mine, outgoing, held, weight, total, left, right, in_sem, own_sem = scratch[11:20]
    links = Links(held, weight, left, right, scratch[20:])
    mp = links.mp

    def fetch(q):
        return pltpu.make_async_copy(
            projections.at[:, pl.ds(pl.multiple_of(q * WIDE, WIDE), WIDE), :], panels.at[q], in_sem.at[q]
        )

    own = pltpu.make_async_copy(own_weight, links.w_rows(links.y, links.x, None), own_sem)
    links.greet()
    fetch(0).start()
    own.start()
    for q in range(1, CHUNKS):
        fetch(q).start()
    limit = prepare(
        links.seq, mp, offsets, owners, short_filter, long_filter, masks, later, near, taps, pick, product, gated
    )
    own.wait()

    def spill(way, q):
        return links.s_copy(way, q, outgoing.at[q, way])

    def edges(q):
        for way in (0, 1):
            into = (left if way == 0 else right).at[q]
            links.z_take(into, links.sr.at[way, q])
        held[mp, 1, q, 0:SPILL] = mine[0] + left[q]
        held[mp, 1, q, SPILL : 2 * SPILL] = mine[1] + right[q]
        links.z_begin(q, 2)

    def stages(q, segment):
        low, high = SEGMENTS[segment]
        short_stage(mp, q, low, high, panels, near, skip, later, taps, circ, direct, query, product)
        long_stage(low, high, masks, circ, direct, query, product, gated)

    def weight_steps(q, steps):
        for n, step in steps:
            pl.when(q == n)(step)

    def opening(q):
        fetch(q).wait()
        stages(q, 0)
        held[mp, 0, q, 0:SPILL] = place(limit, 2, pick, gated)

    opening(0)
    links.meet()
    links.z_begin(0, 0)
    links.w_begin()

    def chunk(q, _):
        stages(q, 1)
        held[mp, 0, q, SPILL : 2 * SPILL] = place(limit, 3, pick, gated)
        links.z_begin(q, 1)
        stages(q, 2)
        outgoing[q, 0] = place(limit, 5, pick, gated)
        outgoing[q, 1] = place(limit, 0, pick, gated)
        for way in (0, 1):
            spill(way, q).start()
        mine[0] = place(limit, 1, pick, gated)
        mine[1] = place(limit, 4, pick, gated)

        @pl.when(q >= 1)
        def _():
            links.z_first(q - 1, (2,))

        weight_steps(
            q, ((1, links.w_far), (2, lambda: links.w_near(SIDE - 1)), (3, lambda: links.w_near(2)))
        )

        @pl.when(q < CHUNKS - 1)
        def _():
            links.z_first(q, (0, 1))
            opening(q + 1)
            links.z_begin(q + 1, 0)
            edges(q)

        weight_steps(q, ((0, links.w_row), (1, lambda: links.w_near(0)), (2, lambda: links.w_near(1))))
        return 0

    lax.fori_loop(0, CHUNKS, chunk, 0)
    links.z_first(CHUNKS - 1, (0, 1))
    edges(CHUNKS - 1)
    links.z_first(CHUNKS - 1, (2,))
    for n, dx in enumerate((0, SIDE - 1, 1, 2)):
        links.w_last(dx)
        links.relay(0, 2, (n,))
    links.relay(1, 2, range(CHUNKS, PIECES))
    links.relay(0, 2, range(CHUNKS, PIECES))
    links.relay(1, 2, range(CHUNKS))
    links.w_end()
    for half in (0, 1):
        add_product(held, weight, total, mp, half, range(CHUNKS), True)

    def mix(n, _):
        add_sources(held, weight, total, mp, 2 * n + 2, 2 * n + 4)
        for way in (0, 1):
            links.relay(way, 3, (n + way * CHUNKS,))
        return 0

    lax.fori_loop(0, CHUNKS, mix, 0)
    for half in (0, 1):
        for k in (0, 2):
            links.z_arrived(0, 2, k + CHUNKS + half)
            links.z_arrived(1, 2, k + half)
        for d in (3, N_MP - 3):
            add_product(held, weight, total, (mp + d) % N_MP, half, range(CHUNKS))
    far = (mp + N_MP // 2) % N_MP
    for half in (0, 1):
        links.z_arrived(0, 3, half)
        links.z_arrived(1, 3, half + CHUNKS)
        add_product(held, weight, total, far, half, (0, 2))
    for half in (0, 1):
        links.z_arrived(0, 3, 2 + half)
        links.z_arrived(1, 3, 2 + half + CHUNKS)
        finish(held, weight, total, out, far, half, (1, 3))
    links.leave()


FILTER_SCRATCH = [
    pltpu.VMEM((CHUNKS, 3, WIDE, CAP), BF16),
    pltpu.VMEM((BLOCKS, 2 * LONG, LONG), BF16),
    pltpu.VMEM((SHORT - 1, 8, CAP), F32),
    pltpu.VMEM((3, WIDE, WIDE), F32),
    pltpu.VMEM((CHUNKS * GROUPS, LONG), F32),
    pltpu.VMEM((SPILL, 3 * SPILL), BF16),
    pltpu.VMEM((GROUPS, LONG, LONG), BF16),
    pltpu.VMEM((WIDE, WIDE), F32),
    pltpu.VMEM((WIDE, CAP), BF16),
    pltpu.VMEM((WIDE, LONG + CAP), BF16),
    pltpu.VMEM((WIDE, REACH + CAP), BF16),
    pltpu.VMEM((2, SPILL, WIDE), BF16),
    pltpu.VMEM((CHUNKS, 2, SPILL, WIDE), BF16),
]
LINK_SCRATCH = [
    pltpu.VMEM((N_MP, 2, CHUNKS, HALF, WIDE), BF16),
    pltpu.VMEM((N_MP * DEPTH, COLS), BF16),
    pltpu.VMEM((2, HALF, COLS), F32),
    pltpu.VMEM((CHUNKS, SPILL, WIDE), BF16),
    pltpu.VMEM((CHUNKS, SPILL, WIDE), BF16),
    pltpu.SemaphoreType.DMA((CHUNKS,)),
    pltpu.SemaphoreType.DMA,
    pltpu.SemaphoreType.DMA((2, 2)),
    pltpu.SemaphoreType.DMA((2, CHUNKS, 3)),
    pltpu.SemaphoreType.DMA((2, 3, PIECES)),
    pltpu.SemaphoreType.DMA,
    pltpu.SemaphoreType.DMA((2, 2)),
    pltpu.SemaphoreType.DMA((2, 2, SIDE)),
    pltpu.SemaphoreType.DMA((SIDE, SIDE)),
    pltpu.SemaphoreType.DMA,
    pltpu.SemaphoreType.DMA((2, CHUNKS)),
]


def per_device(projections, lengths, owners, offsets, short_filter, long_filter, skip, out_weight):
    vmem = pl.BlockSpec(memory_space=pltpu.VMEM)
    anywhere = pl.BlockSpec(memory_space=pl.ANY)
    return pl.pallas_call(
        mix_kernel,
        out_shape=pltpu.VMEM((TOK, COLS), BF16),
        in_specs=[anywhere, anywhere] + [vmem] * 5,
        out_specs=vmem,
        scratch_shapes=FILTER_SCRATCH + LINK_SCRATCH,
        compiler_params=pltpu.CompilerParams(
            collective_id=0, has_side_effects=True, vmem_limit_bytes=60 * 2**20
        ),
    )(
        projections,
        out_weight,
        offsets.reshape(1, -1),
        owners.reshape(1, -1),
        short_filter.transpose(0, 2, 1),
        long_filter,
        skip.reshape(-1, WIDE),
    )


def solution(mesh):
    placed = (P(None, "mp", "seq"), P(), P(), P(), P(), P(), P(), P("seq", "mp"))
    return jax.shard_map(
        per_device, mesh=mesh, in_specs=placed, out_specs=P("seq", "mp"), check_vma=False
    )
```

time: 106 us -> 99.1 us (0.935)
  the two profiles are of different devices: /device:TPU:64 before, /device:TPU:1 now
where the time goes in v3:
time: 99.1 us; the launch traced here: 97.7 us
  Pallas kernels  96.4 us (97%)
  local copies, waits for them, and re-layouts  1.32 us (1%)
    pallas_call x1, Pallas kernels, per_device(): pl.pallas_call(mix_kernel, out_shape=pltpu.VMEM((TOK, COLS), BF16), in_sp...  96.4 us

profile of v3, /device:TPU:1, one launch (start us, length us, event | category | flops | bytes accessed | tf_op | source)
XLA Modules:
  0.0 97.7 jit_solution(7058255596581219622)
XLA Ops:
  0.0 96.4 %shard_map.73 = bf16[1024,1024]{1,0:T(8,128)(2,1)S(1)} custom-call(bf16[3,512,1536]{2,1,0:T(8,128)(2,1)} %projections.1, bf16[128,1024]{1,0:T(8,128)(2,1)} %own_weight.1, s32[1,128]{1,0:T(1,128)} %bitcast.6, s32[1,128]{1,0:T(1,128)} %bitcast.7, f32[3,7,256]{2,1,0:T(8,128)} %bitcast.4, bf16[256,128]{1,0:T(8,128)(2,1)} %long_filter.1, f32[32,128]{1,0:T(8,128)} %bitcast.5), custom_call_target="tpu_custom_call" | custom-call | tf_op jit(solution)/shard_map/pallas_call | solution.py:538
  96.4 1.3 %copy.9 = bf16[1024,1024]{1,0:T(8,128)(2,1)} copy(bf16[1024,1024]{1,0:T(8,128)(2,1)S(1)} %shard_map.73) | data formatting | bytes 4194304

commit v4 on v3

--- a/solution.py
+++ b/solution.py
@@ -22,25 +22,31 @@
 CHUNKS = 4
 GROUPS = WIDE // GSIZE
 BLOCKS = CAP // LONG
-REACH = 2 * SPILL
+PAD = 2 * SPILL // LONG
 
 
 def iota(shape, dim):
     return lax.broadcasted_iota(jnp.int32, shape, dim)
 
 
-def prepare(seq, model, offsets, owners, short_filter, long_filter, masks, later, near, taps, pick, product, gated):
+def owner_span(seq, offsets, owners):
     off = offsets[...]
     own = owners[...]
     first = jnp.min(jnp.where(own == seq, off, TOKENS), axis=1, keepdims=True)
     after = jnp.min(jnp.where(own == seq + 1, off, TOKENS), axis=1, keepdims=True)
     shift = first - seq * TOK + SPILL
-    column = jnp.broadcast_to(off, (LONG, LONG)).T
+    steps = lax.shift_right_arithmetic(shift, 7)
+    coarse = steps * LONG
+    return first - coarse, steps, shift - coarse, after - first + shift
+
+
+def mark_blocks(start, blocks, offsets, masks, later):
+    column = jnp.broadcast_to(offsets[...], (LONG, LONG)).T
     lag = iota((LONG, LONG), 1) - iota((LONG, LONG), 0)
     older = jnp.where(lag < 0, lag + LONG, TOKENS)
     newer = jnp.where(lag >= 0, lag, TOKENS)
-    for b in range(BLOCKS):
-        token = first + iota((1, LONG), 1) + b * LONG
+    for b in blocks:
+        token = start + iota((1, LONG), 1) + b * LONG
         begin = jnp.max(jnp.where(column <= token, column, 0), axis=0, keepdims=True)
         pos = jnp.broadcast_to(token - begin, (8, LONG))
         wide = jnp.broadcast_to(token - begin, (LONG, LONG))
@@ -48,89 +54,106 @@
         masks[b, LONG : 2 * LONG, :] = jnp.where(newer <= wide, 1.0, 0.0).astype(BF16)
         for j in range(1, SHORT):
             later[j - 1, :, b * LONG : (b + 1) * LONG] = jnp.where(pos >= j, 1.0, 0.0)
+
+
+def prepare(model, fine, short_filter, long_filter, near, taps, pick, product, gated):
     rows = CHUNKS * GROUPS
     taps[...] = long_filter[pl.ds(pl.multiple_of(model * rows, rows), rows), :].astype(F32)
     aside = pl.ds(pl.multiple_of(model // 4 * WIDE, WIDE), WIDE)
     for p in range(3):
         block = jnp.concatenate([short_filter[p, :, aside], jnp.zeros((WIDE - SHORT, WIDE), F32)], axis=0)
         near[p] = block.T
-    turned = iota((SPILL, 3 * SPILL), 1) - iota((SPILL, 3 * SPILL), 0) - REACH
-    pick[...] = jnp.where(turned == -shift, 1.0, 0.0).astype(BF16)
-    product[:, 0:LONG] = jnp.zeros((WIDE, LONG), BF16)
-    gated[:, 0:REACH] = jnp.zeros((WIDE, REACH), BF16)
-    return after - first + shift
-
-
-def short_stage(model, chunk, low_block, high_block, panels, near, skip, later, taps, circ, direct, query, product):
-    row = model % 4 * (CHUNKS * GROUPS) + chunk * GROUPS
-    if low_block == 0:
+    turned = iota((SPILL, 3 * LONG), 1) - iota((SPILL, 3 * LONG), 0) - LONG
+    pick[...] = jnp.where(turned == -fine, 1.0, 0.0).astype(BF16)
+    product[:, :, 0:LONG] = jnp.zeros((CHUNKS, WIDE, LONG), BF16)
+    gated[:, :, 0:LONG] = jnp.zeros((CHUNKS, WIDE, LONG), BF16)
+
+
+def short_stage(model, chunk, ranges, fresh, coarse, panels, near, factors, skip, later, taps, circ, direct, query, product):
+    if fresh:
         gains = skip[pl.ds(model * CHUNKS + chunk, 1), :]
-        direct[...] = jnp.broadcast_to(gains, (WIDE, WIDE)).T
+        direct[chunk] = jnp.broadcast_to(gains, (WIDE, WIDE)).T
+        first_row = pl.multiple_of(model % 4 * (CHUNKS * GROUPS) + chunk * GROUPS, GROUPS)
+        for p in range(3):
+            mine = near[p, pl.ds(first_row, GROUPS), :]
+            for j in range(SHORT):
+                factors[chunk, p * SHORT + j] = jnp.broadcast_to(mine[:, j : j + 1], (GROUPS, WIDE))
     lane = iota((GSIZE, LONG), 1)
+    steps = jnp.broadcast_to(coarse, (GSIZE, LONG))
 
     def short(g, _):
         ch = pl.ds(pl.multiple_of(g * GSIZE, GSIZE), GSIZE)
-        if low_block == 0:
-            line = jnp.broadcast_to(taps[pl.ds(chunk * GROUPS + g, 1), :], (LONG, LONG))
-            circ[g] = pltpu.roll(line, 0, 1, stride=1, stride_axis=0).astype(BF16)
-        factor = []
-        for p in range(3):
-            f = near[p, pl.ds(row + g, 1), :]
-            factor.append([jnp.broadcast_to(f[:, j : j + 1], (8, LONG)) for j in range(SHORT)])
-        rolled = [[None] * SHORT for _ in range(3)]
-        if low_block > 0:
-            at = slice((low_block - 1) * LONG, low_block * LONG)
-            rolled = [[pltpu.roll(panels[chunk, p, ch, at], j, 1) for j in range(SHORT)] for p in range(3)]
-        for b in range(low_block, high_block):
-            at = slice(b * LONG, (b + 1) * LONG)
-            sums = []
-            for p in range(3):
-                x = panels[chunk, p, ch, at]
-                wide = x.astype(F32)
-                low = factor[p][0] * wide[0:8]
-                high = factor[p][0] * wide[8:16]
-                for j in range(1, SHORT):
-                    turned = pltpu.roll(x, j, 1)
-                    before = rolled[p][j]
-                    rolled[p][j] = turned
-                    if b > 0:
-                        turned = jnp.where(lane < j, before, turned)
-                    weight = factor[p][j] * later[j - 1, :, at]
-                    wide = turned.astype(F32)
-                    low = low + weight * wide[0:8]
-                    high = high + weight * wide[8:16]
-                sums.append(jnp.concatenate([low, high], axis=0))
-            query[ch, at] = sums[0].astype(BF16)
-            product[ch, (b + 1) * LONG : (b + 2) * LONG] = (sums[1] * sums[2]).astype(BF16)
+        row = chunk * GROUPS + g
+
+        def cells(p, b):
+            x = panels[chunk, p, ch, (b + PAD) * LONG : (b + PAD + 1) * LONG]
+            for k in range(1, PAD + 1):
+                at = (b + PAD - k) * LONG
+                x = jnp.where(steps == k, panels[chunk, p, ch, at : at + LONG], x)
+            return x
+
+        if fresh:
+            line = jnp.broadcast_to(taps[pl.ds(row, 1), :], (LONG, LONG))
+            circ[chunk, g] = pltpu.roll(line, 0, 1, stride=1, stride_axis=0).astype(BF16)
+        factor = [
+            [jnp.broadcast_to(factors[chunk, p * SHORT + j, pl.ds(g, 1), :], (8, LONG)) for j in range(SHORT)]
+            for p in range(3)
+        ]
+        for low_block, high_block in ranges:
+            rolled = [[None] * SHORT for _ in range(3)]
+            if low_block > 0:
+                before = [cells(p, low_block - 1) for p in range(3)]
+                rolled = [[pltpu.roll(before[p], j, 1) for j in range(SHORT)] for p in range(3)]
+            for b in range(low_block, high_block):
+                at = slice(b * LONG, (b + 1) * LONG)
+                sums = []
+                for p in range(3):
+                    x = cells(p, b)
+                    wide = x.astype(F32)
+                    low = factor[p][0] * wide[0:8]
+                    high = factor[p][0] * wide[8:16]
+                    for j in range(1, SHORT):
+                        turned = pltpu.roll(x, j, 1)
+                        before = rolled[p][j]
+                        rolled[p][j] = turned
+                        if b > 0:
+                            turned = jnp.where(lane < j, before, turned)
+                        weight = factor[p][j] * later[j - 1, :, at]
+                        wide = turned.astype(F32)
+                        low = low + weight * wide[0:8]
+                        high = high + weight * wide[8:16]
+                    sums.append(jnp.concatenate([low, high], axis=0))
+                query[chunk, ch, at] = sums[0].astype(BF16)
+                product[chunk, ch, (b + 1) * LONG : (b + 2) * LONG] = (sums[1] * sums[2]).astype(BF16)
         return 0
 
     lax.fori_loop(0, GROUPS, short, 0)
 
 
-def long_stage(low_block, high_block, masks, circ, direct, query, product, gated):
+def long_stage(chunk, low_block, high_block, masks, circ, direct, query, product, gated):
     def long(b, _):
         at = pl.multiple_of(b * LONG, LONG)
         older = masks[b, 0:LONG, :]
         newer = masks[b, LONG : 2 * LONG, :]
         for g in range(GROUPS):
             ch = slice(g * GSIZE, (g + 1) * GSIZE)
-            matrix = jnp.concatenate([circ[g] * older, circ[g] * newer], axis=0)
-            window = product[ch, pl.ds(at, 2 * LONG)]
+            matrix = jnp.concatenate([circ[chunk, g] * older, circ[chunk, g] * newer], axis=0)
+            window = product[chunk, ch, pl.ds(at, 2 * LONG)]
             w = jnp.dot(window, matrix, preferred_element_type=F32)
-            now = product[ch, pl.ds(at + LONG, LONG)].astype(F32)
-            w = w + direct[ch, :] * now
-            out = query[ch, pl.ds(at, LONG)].astype(F32) * w
-            gated[ch, pl.ds(at + REACH, LONG)] = out.astype(BF16)
+            now = product[chunk, ch, pl.ds(at + LONG, LONG)].astype(F32)
+            w = w + direct[chunk, ch, :] * now
+            out = query[chunk, ch, pl.ds(at, LONG)].astype(F32) * w
+            gated[chunk, ch, pl.ds(at + LONG, LONG)] = out.astype(BF16)
         return 0
 
     lax.fori_loop(low_block, high_block, long, 0)
 
 
-def place(limit, k, pick, gated):
+def place(limit, chunk, k, pick, gated):
     at = k * SPILL
     if not isinstance(k, int):
         at = pl.multiple_of(at, SPILL)
-    block = gated[:, pl.ds(at, 3 * SPILL)]
+    block = gated[chunk, :, pl.ds(at, 3 * LONG)]
     moved = lax.dot_general(
         pick[...], block, (((1,), (1,)), ((), ())), preferred_element_type=F32
     )
@@ -191,18 +214,16 @@
 
     def z_begin(self, chunk, part):
         for way in (0, 1):
-            self.z_push(way, self.own_part(self.mp, chunk, part), self.zf.at[way, chunk, part])
+            self.z_push(way, self.own_part(self.mp, chunk, part), self.zf.at[way, chunk, part // 2])
 
     def behind(self, way, step):
         return (self.mp + (N_MP - step if way == 0 else step)) % N_MP
 
-    def z_first(self, chunk, parts):
-        for way in (0, 1):
-            src = self.behind(way, 1)
-            for part in parts:
-                self.z_take(self.own_part(src, chunk, part), self.zf.at[way, chunk, part])
-            half = parts[-1] // 2
-            self.z_push(way, self.held.at[src, half, chunk], self.zr.at[way, 0, 2 * chunk + half])
+    def z_first(self, chunk, half):
+        for way in (0, 1):
+            ref = self.held.at[self.behind(way, 1), half, chunk]
+            self.z_take(ref, self.zf.at[way, chunk, half])
+            self.z_push(way, ref, self.zr.at[way, 0, 2 * chunk + half])
 
     def z_ref(self, way, step, piece):
         return self.held.at[self.behind(way, step + 1), piece % 2, piece // 2]
@@ -254,13 +275,8 @@
     def c_copy(self, dy, dx):
         ref = self.w_rows(self.y + dy, self.x + dx, None)
         return self.w_copy(
-            self.ws, self.cr.at[dy, dx], ref, seq_at(self.y, self.x, 1 - self.core)
-        )
-
-    def c_arrived(self, dy, dx):
-        at = seq_at(self.y + dy, self.x + dx, 1 - self.core) * ROWS_W
-        ref = self.weight.at[pl.ds(pl.multiple_of(at, ROWS_W), ROWS_W), :]
-        self.z_take(ref, self.cr.at[dy, dx])
+            self.ws, self.cr, ref, seq_at(self.y, self.x, 1 - self.core)
+        )
 
     def s_copy(self, way, chunk, ref):
         into = (self.left if way == 0 else self.right).at[chunk]
@@ -303,9 +319,7 @@
         self.c_copy(2, dx).start()
 
     def w_end(self):
-        for dy in range(SIDE):
-            for dx in range(SIDE):
-                self.c_arrived(dy, dx)
+        self.z_take(self.weight.at[0 : SIDE * SIDE * ROWS_W], self.cr)
 
     def leave(self):
         for way in (0, 1):
@@ -373,18 +387,24 @@
     lax.fori_loop(low, high, body, 0)
 
 
-SEGMENTS = ((0, 6), (6, 8), (8, BLOCKS))
+SEGMENTS = (
+    (((2, 6),), ((3, 6),)),
+    (((6, 8),), ((6, 8),)),
+    (((0, 2), (8, BLOCKS)), ((0, 3), (8, BLOCKS))),
+)
 
 
 def mix_kernel(projections, own_weight, offsets, owners, short_filter, long_filter, skip, out, *scratch):
-    panels, masks, later, near, taps, pick, circ, direct, query, product, gated = scratch[:11]
-    mine, outgoing, held, weight, total, left, right, in_sem, own_sem = scratch[11:20]
-    links = Links(held, weight, left, right, scratch[20:])
+    panels, masks, later, near, factors, taps, pick, circ, direct, query, product, gated = scratch[:12]
+    mine, outgoing, held, weight, total, left, right, in_sem, own_sem = scratch[12:21]
+    links = Links(held, weight, left, right, scratch[21:])
     mp = links.mp
 
     def fetch(q):
         return pltpu.make_async_copy(
-            projections.at[:, pl.ds(pl.multiple_of(q * WIDE, WIDE), WIDE), :], panels.at[q], in_sem.at[q]
+            projections.at[:, pl.ds(pl.multiple_of(q * WIDE, WIDE), WIDE), :],
+            panels.at[q, :, :, PAD * LONG :],
+            in_sem.at[q],
         )
 
     own = pltpu.make_async_copy(own_weight, links.w_rows(links.y, links.x, None), own_sem)
@@ -393,10 +413,14 @@
     own.start()
     for q in range(1, CHUNKS):
         fetch(q).start()
-    limit = prepare(
-        links.seq, mp, offsets, owners, short_filter, long_filter, masks, later, near, taps, pick, product, gated
-    )
+    start, coarse, fine, limit = owner_span(links.seq, offsets, owners)
+    clear = jnp.zeros((3, WIDE, PAD * LONG), BF16)
+    panels[0, :, :, 0 : PAD * LONG] = clear
+    prepare(mp, fine, short_filter, long_filter, near, taps, pick, product, gated)
+    mark_blocks(start, range(2, 6), offsets, masks, later)
     own.wait()
+    for q in range(CHUNKS):
+        fetch(q).wait()
 
     def spill(way, q):
         return links.s_copy(way, q, outgoing.at[q, way])
@@ -405,111 +429,148 @@
         for way in (0, 1):
             into = (left if way == 0 else right).at[q]
             links.z_take(into, links.sr.at[way, q])
-        held[mp, 1, q, 0:SPILL] = mine[0] + left[q]
-        held[mp, 1, q, SPILL : 2 * SPILL] = mine[1] + right[q]
+        held[mp, 1, q, 0:SPILL] = mine[q, 0] + left[q]
+        held[mp, 1, q, SPILL : 2 * SPILL] = mine[q, 1] + right[q]
         links.z_begin(q, 2)
 
     def stages(q, segment):
-        low, high = SEGMENTS[segment]
-        short_stage(mp, q, low, high, panels, near, skip, later, taps, circ, direct, query, product)
-        long_stage(low, high, masks, circ, direct, query, product, gated)
-
-    def weight_steps(q, steps):
+        short_ranges, long_ranges = SEGMENTS[segment]
+        short_stage(
+            mp, q, short_ranges, segment == 0, coarse, panels, near, factors, skip, later, taps, circ, direct, query, product
+        )
+        for low, high in long_ranges:
+            long_stage(q, low, high, masks, circ, direct, query, product, gated)
+
+    def second(piece):
+        for way in (0, 1):
+            links.relay(way, 2, (piece,))
+
+    def at_chunk(q, steps):
         for n, step in steps:
             pl.when(q == n)(step)
 
     def opening(q):
-        fetch(q).wait()
         stages(q, 0)
-        held[mp, 0, q, 0:SPILL] = place(limit, 2, pick, gated)
+        held[mp, 0, q, 0:SPILL] = place(limit, q, 2, pick, gated)
 
     opening(0)
     links.meet()
     links.z_begin(0, 0)
     links.w_begin()
-
-    def chunk(q, _):
+    mark_blocks(start, (6, 7), offsets, masks, later)
+
+    def middle(q, _):
         stages(q, 1)
-        held[mp, 0, q, SPILL : 2 * SPILL] = place(limit, 3, pick, gated)
+        held[mp, 0, q, SPILL : 2 * SPILL] = place(limit, q, 3, pick, gated)
         links.z_begin(q, 1)
+
+        @pl.when(q < CHUNKS - 1)
+        def _():
+            panels[q + 1, :, :, 0 : PAD * LONG] = clear
+            opening(q + 1)
+            links.z_begin(q + 1, 0)
+
+        at_chunk(
+            q,
+            (
+                (0, lambda: links.z_first(0, 0)),
+                (1, links.w_row),
+                (2, lambda: links.z_first(1, 0)),
+                (3, lambda: links.z_first(2, 0)),
+                (3, links.w_far),
+                (3, lambda: links.w_near(0)),
+            ),
+        )
+        return 0
+
+    lax.fori_loop(0, CHUNKS, middle, 0)
+    mark_blocks(start, (0, 1, 8, 9, 10, 11), offsets, masks, later)
+
+    def outer(q, _):
         stages(q, 2)
-        outgoing[q, 0] = place(limit, 5, pick, gated)
-        outgoing[q, 1] = place(limit, 0, pick, gated)
+        outgoing[q, 0] = place(limit, q, 5, pick, gated)
+        outgoing[q, 1] = place(limit, q, 0, pick, gated)
         for way in (0, 1):
             spill(way, q).start()
-        mine[0] = place(limit, 1, pick, gated)
-        mine[1] = place(limit, 4, pick, gated)
-
+        mine[q, 0] = place(limit, q, 1, pick, gated)
+        mine[q, 1] = place(limit, q, 4, pick, gated)
         @pl.when(q >= 1)
         def _():
-            links.z_first(q - 1, (2,))
-
-        weight_steps(
-            q, ((1, links.w_far), (2, lambda: links.w_near(SIDE - 1)), (3, lambda: links.w_near(2)))
-        )
-
-        @pl.when(q < CHUNKS - 1)
-        def _():
-            links.z_first(q, (0, 1))
-            opening(q + 1)
-            links.z_begin(q + 1, 0)
-            edges(q)
-
-        weight_steps(q, ((0, links.w_row), (1, lambda: links.w_near(0)), (2, lambda: links.w_near(1))))
+            edges(q - 1)
+
+        at_chunk(
+            q,
+            (
+                (0, lambda: second(0)),
+                (1, lambda: links.z_first(3, 0)),
+                (2, lambda: second(2)),
+                (3, lambda: links.z_first(0, 1)),
+                (0, lambda: links.w_near(SIDE - 1)),
+                (1, lambda: links.w_near(1)),
+                (2, lambda: links.w_near(2)),
+            ),
+        )
         return 0
 
-    lax.fori_loop(0, CHUNKS, chunk, 0)
-    links.z_first(CHUNKS - 1, (0, 1))
+    lax.fori_loop(0, CHUNKS, outer, 0)
     edges(CHUNKS - 1)
-    links.z_first(CHUNKS - 1, (2,))
-    for n, dx in enumerate((0, SIDE - 1, 1, 2)):
-        links.w_last(dx)
-        links.relay(0, 2, (n,))
-    links.relay(1, 2, range(CHUNKS, PIECES))
-    links.relay(0, 2, range(CHUNKS, PIECES))
-    links.relay(1, 2, range(CHUNKS))
+    links.w_last(0)
+    links.w_last(SIDE - 1)
+    links.z_first(1, 1)
+    links.w_last(1)
+    links.w_last(2)
     links.w_end()
     for half in (0, 1):
         add_product(held, weight, total, mp, half, range(CHUNKS), True)
-
-    def mix(n, _):
-        add_sources(held, weight, total, mp, 2 * n + 2, 2 * n + 4)
-        for way in (0, 1):
-            links.relay(way, 3, (n + way * CHUNKS,))
-        return 0
-
-    lax.fori_loop(0, CHUNKS, mix, 0)
+    links.z_first(2, 1)
+    links.z_first(3, 1)
+    second(4)
+    second(6)
+    add_sources(held, weight, total, mp, 2, 4)
+    second(1)
+    add_sources(held, weight, total, mp, 4, 6)
+    for k in (3, 5, 7):
+        second(k)
+    add_sources(held, weight, total, mp, 6, 10)
     for half in (0, 1):
-        for k in (0, 2):
-            links.z_arrived(0, 2, k + CHUNKS + half)
-            links.z_arrived(1, 2, k + half)
+        for k in (0, 1):
+            links.relay(0, 3, (2 * k + half,))
+            links.z_arrived(1, 2, 2 * k + half)
+        for k in (2, 3):
+            links.relay(1, 3, (2 * k + half,))
+            links.z_arrived(0, 2, 2 * k + half)
         for d in (3, N_MP - 3):
             add_product(held, weight, total, (mp + d) % N_MP, half, range(CHUNKS))
     far = (mp + N_MP // 2) % N_MP
-    for half in (0, 1):
-        links.z_arrived(0, 3, half)
-        links.z_arrived(1, 3, half + CHUNKS)
-        add_product(held, weight, total, far, half, (0, 2))
-    for half in (0, 1):
-        links.z_arrived(0, 3, 2 + half)
-        links.z_arrived(1, 3, 2 + half + CHUNKS)
-        finish(held, weight, total, out, far, half, (1, 3))
+
+    def last(half, k):
+        links.z_arrived(0, 3, 2 * k + half)
+        links.z_arrived(1, 3, 2 * (k + 2) + half)
+
+    last(0, 0)
+    last(0, 1)
+    finish(held, weight, total, out, far, 0, range(CHUNKS))
+    last(1, 0)
+    add_product(held, weight, total, far, 1, (0, 2))
+    last(1, 1)
+    finish(held, weight, total, out, far, 1, (1, 3))
     links.leave()
 
 
 FILTER_SCRATCH = [
-    pltpu.VMEM((CHUNKS, 3, WIDE, CAP), BF16),
+    pltpu.VMEM((CHUNKS, 3, WIDE, PAD * LONG + CAP), BF16),
     pltpu.VMEM((BLOCKS, 2 * LONG, LONG), BF16),
     pltpu.VMEM((SHORT - 1, 8, CAP), F32),
     pltpu.VMEM((3, WIDE, WIDE), F32),
+    pltpu.VMEM((CHUNKS, 3 * SHORT, GROUPS, WIDE), F32),
     pltpu.VMEM((CHUNKS * GROUPS, LONG), F32),
-    pltpu.VMEM((SPILL, 3 * SPILL), BF16),
-    pltpu.VMEM((GROUPS, LONG, LONG), BF16),
-    pltpu.VMEM((WIDE, WIDE), F32),
-    pltpu.VMEM((WIDE, CAP), BF16),
-    pltpu.VMEM((WIDE, LONG + CAP), BF16),
-    pltpu.VMEM((WIDE, REACH + CAP), BF16),
-    pltpu.VMEM((2, SPILL, WIDE), BF16),
+    pltpu.VMEM((SPILL, 3 * LONG), BF16),
+    pltpu.VMEM((CHUNKS, GROUPS, LONG, LONG), BF16),
+    pltpu.VMEM((CHUNKS, WIDE, WIDE), F32),
+    pltpu.VMEM((CHUNKS, WIDE, CAP), BF16),
+    pltpu.VMEM((CHUNKS, WIDE, LONG + CAP), BF16),
+    pltpu.VMEM((CHUNKS, WIDE, LONG + CAP), BF16),
+    pltpu.VMEM((CHUNKS, 2, SPILL, WIDE), BF16),
     pltpu.VMEM((CHUNKS, 2, SPILL, WIDE), BF16),
 ]
 LINK_SCRATCH = [
@@ -521,12 +582,12 @@
     pltpu.SemaphoreType.DMA((CHUNKS,)),
     pltpu.SemaphoreType.DMA,
     pltpu.SemaphoreType.DMA((2, 2)),
-    pltpu.SemaphoreType.DMA((2, CHUNKS, 3)),
+    pltpu.SemaphoreType.DMA((2, CHUNKS, 2)),
     pltpu.SemaphoreType.DMA((2, 3, PIECES)),
     pltpu.SemaphoreType.DMA,
     pltpu.SemaphoreType.DMA((2, 2)),
     pltpu.SemaphoreType.DMA((2, 2, SIDE)),
-    pltpu.SemaphoreType.DMA((SIDE, SIDE)),
+    pltpu.SemaphoreType.DMA,
     pltpu.SemaphoreType.DMA,
     pltpu.SemaphoreType.DMA((2, CHUNKS)),
 ]

time: 99.1 us -> 97.4 us (0.983); the launches traced: 97.7 us -> 97.3 us
  no operation moved by 1% of the time
where the time goes in v4:
time: 97.4 us; the launch traced here: 97.3 us
  Pallas kernels  96 us (99%)
  local copies, waits for them, and re-layouts  1.32 us (1%)
    pallas_call x1, Pallas kernels, per_device(): pl.pallas_call(mix_kernel, out_shape=pltpu.VMEM((TOK, COLS), BF16), in_sp...  96 us

profile of v4, /device:TPU:1, one launch (start us, length us, event | category | flops | bytes accessed | tf_op | source)
XLA Modules:
  0.0 97.3 jit_solution(13502123377175648032)
XLA Ops:
  0.0 96.0 %shard_map.73 = bf16[1024,1024]{1,0:T(8,128)(2,1)S(1)} custom-call(bf16[3,512,1536]{2,1,0:T(8,128)(2,1)} %projections.1, bf16[128,1024]{1,0:T(8,128)(2,1)} %own_weight.1, s32[1,128]{1,0:T(1,128)} %bitcast.6, s32[1,128]{1,0:T(1,128)} %bitcast.7, f32[3,7,256]{2,1,0:T(8,128)} %bitcast.4, bf16[256,128]{1,0:T(8,128)(2,1)} %long_filter.1, f32[32,128]{1,0:T(8,128)} %bitcast.5), custom_call_target="tpu_custom_call" | custom-call | tf_op jit(solution)/shard_map/pallas_call | solution.py:599
  96.0 1.3 %copy.9 = bf16[1024,1024]{1,0:T(8,128)(2,1)} copy(bf16[1024,1024]{1,0:T(8,128)(2,1)S(1)} %shard_map.73) | data formatting | bytes 4194304

commit v5 on v4

--- a/solution.py
+++ b/solution.py
@@ -40,7 +40,7 @@
     return first - coarse, steps, shift - coarse, after - first + shift
 
 
-def mark_blocks(start, blocks, offsets, masks, later):
+def mark_blocks(start, blocks, offsets, masks, later, bare=()):
     column = jnp.broadcast_to(offsets[...], (LONG, LONG)).T
     lag = iota((LONG, LONG), 1) - iota((LONG, LONG), 0)
     older = jnp.where(lag < 0, lag + LONG, TOKENS)
@@ -50,13 +50,14 @@
         begin = jnp.max(jnp.where(column <= token, column, 0), axis=0, keepdims=True)
         pos = jnp.broadcast_to(token - begin, (8, LONG))
         wide = jnp.broadcast_to(token - begin, (LONG, LONG))
-        masks[b, 0:LONG, :] = jnp.where(older <= wide, 1.0, 0.0).astype(BF16)
-        masks[b, LONG : 2 * LONG, :] = jnp.where(newer <= wide, 1.0, 0.0).astype(BF16)
+        if b not in bare:
+            masks[b, 0:LONG, :] = jnp.where(older <= wide, 1.0, 0.0).astype(BF16)
+            masks[b, LONG : 2 * LONG, :] = jnp.where(newer <= wide, 1.0, 0.0).astype(BF16)
         for j in range(1, SHORT):
             later[j - 1, :, b * LONG : (b + 1) * LONG] = jnp.where(pos >= j, 1.0, 0.0)
 
 
-def prepare(model, fine, short_filter, long_filter, near, taps, pick, product, gated):
+def prepare(model, fine, short_filter, long_filter, near, taps, pick):
     rows = CHUNKS * GROUPS
     taps[...] = long_filter[pl.ds(pl.multiple_of(model * rows, rows), rows), :].astype(F32)
     aside = pl.ds(pl.multiple_of(model // 4 * WIDE, WIDE), WIDE)
@@ -65,8 +66,6 @@
         near[p] = block.T
     turned = iota((SPILL, 3 * LONG), 1) - iota((SPILL, 3 * LONG), 0) - LONG
     pick[...] = jnp.where(turned == -fine, 1.0, 0.0).astype(BF16)
-    product[:, :, 0:LONG] = jnp.zeros((CHUNKS, WIDE, LONG), BF16)
-    gated[:, :, 0:LONG] = jnp.zeros((CHUNKS, WIDE, LONG), BF16)
 
 
 def short_stage(model, chunk, ranges, fresh, coarse, panels, near, factors, skip, later, taps, circ, direct, query, product):
@@ -213,8 +212,11 @@
         return self.held.at[src, 0, chunk, part * SPILL : (part + 1) * SPILL]
 
     def z_begin(self, chunk, part):
-        for way in (0, 1):
-            self.z_push(way, self.own_part(self.mp, chunk, part), self.zf.at[way, chunk, part // 2])
+        slot = part // 2
+        if part == 1:
+            slot = (CHUNKS - chunk) // CHUNKS * 2
+        for way in (0, 1):
+            self.z_push(way, self.own_part(self.mp, chunk, part), self.zf.at[way, chunk, slot])
 
     def behind(self, way, step):
         return (self.mp + (N_MP - step if way == 0 else step)) % N_MP
@@ -224,6 +226,12 @@
             ref = self.held.at[self.behind(way, 1), half, chunk]
             self.z_take(ref, self.zf.at[way, chunk, half])
             self.z_push(way, ref, self.zr.at[way, 0, 2 * chunk + half])
+
+    def z_half(self, part):
+        for way in (0, 1):
+            ref = self.own_part(self.behind(way, 1), 0, part)
+            self.z_take(ref, self.zf.at[way, 0, 2 * part])
+            self.z_push(way, ref, self.zr.at[way, 0, 0])
 
     def z_ref(self, way, step, piece):
         return self.held.at[self.behind(way, step + 1), piece % 2, piece // 2]
@@ -415,12 +423,11 @@
         fetch(q).start()
     start, coarse, fine, limit = owner_span(links.seq, offsets, owners)
     clear = jnp.zeros((3, WIDE, PAD * LONG), BF16)
-    panels[0, :, :, 0 : PAD * LONG] = clear
-    prepare(mp, fine, short_filter, long_filter, near, taps, pick, product, gated)
-    mark_blocks(start, range(2, 6), offsets, masks, later)
+    panels[0, :, :, LONG : PAD * LONG] = clear[:, :, LONG:]
+    prepare(mp, fine, short_filter, long_filter, near, taps, pick)
+    mark_blocks(start, range(2, 6), offsets, masks, later, (2,))
     own.wait()
-    for q in range(CHUNKS):
-        fetch(q).wait()
+    fetch(0).wait()
 
     def spill(way, q):
         return links.s_copy(way, q, outgoing.at[q, way])
@@ -433,11 +440,13 @@
         held[mp, 1, q, SPILL : 2 * SPILL] = mine[q, 1] + right[q]
         links.z_begin(q, 2)
 
-    def stages(q, segment):
+    def stages(q, segment, between=None):
         short_ranges, long_ranges = SEGMENTS[segment]
         short_stage(
             mp, q, short_ranges, segment == 0, coarse, panels, near, factors, skip, later, taps, circ, direct, query, product
         )
+        if between is not None:
+            between()
         for low, high in long_ranges:
             long_stage(q, low, high, masks, circ, direct, query, product, gated)
 
@@ -449,14 +458,17 @@
         for n, step in steps:
             pl.when(q == n)(step)
 
-    def opening(q):
-        stages(q, 0)
+    def opening(q, between=None):
+        stages(q, 0, between)
         held[mp, 0, q, 0:SPILL] = place(limit, q, 2, pick, gated)
 
     opening(0)
     links.meet()
     links.z_begin(0, 0)
     links.w_begin()
+    panels[0, :, :, 0:LONG] = clear[:, :, 0:LONG]
+    product[:, :, 0:LONG] = jnp.zeros((CHUNKS, WIDE, LONG), BF16)
+    gated[:, :, 0:LONG] = jnp.zeros((CHUNKS, WIDE, LONG), BF16)
     mark_blocks(start, (6, 7), offsets, masks, later)
 
     def middle(q, _):
@@ -467,13 +479,14 @@
         @pl.when(q < CHUNKS - 1)
         def _():
             panels[q + 1, :, :, 0 : PAD * LONG] = clear
-            opening(q + 1)
+            fetch(q + 1).wait()
+            opening(q + 1, lambda: pl.when(q == 0)(lambda: links.z_half(0)))
             links.z_begin(q + 1, 0)
 
         at_chunk(
             q,
             (
-                (0, lambda: links.z_first(0, 0)),
+                (0, lambda: links.z_half(1)),
                 (1, links.w_row),
                 (2, lambda: links.z_first(1, 0)),
                 (3, lambda: links.z_first(2, 0)),
@@ -484,7 +497,7 @@
         return 0
 
     lax.fori_loop(0, CHUNKS, middle, 0)
-    mark_blocks(start, (0, 1, 8, 9, 10, 11), offsets, masks, later)
+    mark_blocks(start, (0, 1, 2, 8, 9, 10, 11), offsets, masks, later)
 
     def outer(q, _):
         stages(q, 2)
@@ -582,7 +595,7 @@
     pltpu.SemaphoreType.DMA((CHUNKS,)),
     pltpu.SemaphoreType.DMA,
     pltpu.SemaphoreType.DMA((2, 2)),
-    pltpu.SemaphoreType.DMA((2, CHUNKS, 2)),
+    pltpu.SemaphoreType.DMA((2, CHUNKS, 3)),
     pltpu.SemaphoreType.DMA((2, 3, PIECES)),
     pltpu.SemaphoreType.DMA,
     pltpu.SemaphoreType.DMA((2, 2)),

time: 97.4 us -> 97.4 us (level)
  no operation moved by 1% of the time
where the time goes in v5:
time: 97.4 us; the launch traced here: 97.3 us
  Pallas kernels  96 us (99%)
  local copies, waits for them, and re-layouts  1.32 us (1%)
    pallas_call x1, Pallas kernels, per_device(): pl.pallas_call(mix_kernel, out_shape=pltpu.VMEM((TOK, COLS), BF16), in_sp...  96 us

profile of v5, /device:TPU:1, one launch (start us, length us, event | category | flops | bytes accessed | tf_op | source)
XLA Modules:
  0.0 97.3 jit_solution(14339435584849175121)
XLA Ops:
  0.0 96.0 %shard_map.73 = bf16[1024,1024]{1,0:T(8,128)(2,1)S(1)} custom-call(bf16[3,512,1536]{2,1,0:T(8,128)(2,1)} %projections.1, bf16[128,1024]{1,0:T(8,128)(2,1)} %own_weight.1, s32[1,128]{1,0:T(1,128)} %bitcast.6, s32[1,128]{1,0:T(1,128)} %bitcast.7, f32[3,7,256]{2,1,0:T(8,128)} %bitcast.4, bf16[256,128]{1,0:T(8,128)(2,1)} %long_filter.1, f32[32,128]{1,0:T(8,128)} %bitcast.5), custom_call_target="tpu_custom_call" | custom-call | tf_op jit(solution)/shard_map/pallas_call | solution.py:612
  96.0 1.3 %copy.9 = bf16[1024,1024]{1,0:T(8,128)(2,1)} copy(bf16[1024,1024]{1,0:T(8,128)(2,1)S(1)} %shard_map.73) | data formatting | bytes 4194304

commit v6 on v5

--- a/solution.py
+++ b/solution.py
@@ -245,6 +245,16 @@
             self.z_arrived(way, step - 1, piece)
             self.z_push(way, self.z_ref(way, step - 1, piece), self.zr.at[way, step - 1, piece], late)
 
+    def relay_last(self, way, piece):
+        self.z_arrived(way, 2, piece)
+        for part in (0, 1):
+            ref = self.z_ref(way, 2, piece).at[part * SPILL : (part + 1) * SPILL]
+            self.z_push(way, ref, self.zr.at[way, 2, (piece + part * CHUNKS) % PIECES], 1)
+
+    def last_arrived(self, way, piece, part):
+        ref = self.z_ref(way, 3, piece).at[part * SPILL : (part + 1) * SPILL]
+        self.z_take(ref, self.zr.at[way, 2, (piece + part * CHUNKS) % PIECES])
+
     def w_rows(self, y, x, part):
         at = seq_at(y, x, self.core) * ROWS_W
         size = ROWS_W
@@ -376,6 +386,23 @@
         else:
             out[0:SPILL, cols] = value[0:SPILL]
             out[TOK - SPILL : TOK, cols] = value[SPILL:]
+        return 0
+
+    lax.fori_loop(0, COLS // COLS_STEP, body, 0)
+
+
+def finish_rows(held, weight, total, out, src, part, chunks):
+    rows = slice(part * SPILL, (part + 1) * SPILL)
+    at = part * (TOK - SPILL)
+
+    def body(n, _):
+        cols = columns(n)
+        lhs = jnp.concatenate([held[src, 1, q, rows] for q in chunks], axis=1)
+        rhs = jnp.concatenate(
+            [weight[pl.ds(pl.multiple_of((src * CHUNKS + q) * WIDE, WIDE), WIDE), cols] for q in chunks], axis=0
+        )
+        value = total[1, rows, cols] + jnp.dot(lhs, rhs, preferred_element_type=F32)
+        out[at : at + SPILL, cols] = value.astype(BF16)
         return 0
 
     lax.fori_loop(0, COLS // COLS_STEP, body, 0)
@@ -547,10 +574,10 @@
     add_sources(held, weight, total, mp, 6, 10)
     for half in (0, 1):
         for k in (0, 1):
-            links.relay(0, 3, (2 * k + half,))
+            (links.relay_last(0, 3) if (k, half) == (1, 1) else links.relay(0, 3, (2 * k + half,)))
             links.z_arrived(1, 2, 2 * k + half)
         for k in (2, 3):
-            links.relay(1, 3, (2 * k + half,))
+            (links.relay_last(1, 7) if (k, half) == (3, 1) else links.relay(1, 3, (2 * k + half,)))
             links.z_arrived(0, 2, 2 * k + half)
         for d in (3, N_MP - 3):
             add_product(held, weight, total, (mp + d) % N_MP, half, range(CHUNKS))
@@ -565,8 +592,10 @@
     finish(held, weight, total, out, far, 0, range(CHUNKS))
     last(1, 0)
     add_product(held, weight, total, far, 1, (0, 2))
-    last(1, 1)
-    finish(held, weight, total, out, far, 1, (1, 3))
+    for part in (0, 1):
+        links.last_arrived(0, 3, part)
+        links.last_arrived(1, 7, part)
+        finish_rows(held, weight, total, out, far, part, (1, 3))
     links.leave()
 
 

time: 97.4 us -> 97.2 us (level)
  no operation moved by 1% of the time
where the time goes in v6:
time: 97.2 us; the launch traced here: 97.1 us
  Pallas kernels  95.8 us (99%)
  local copies, waits for them, and re-layouts  1.32 us (1%)
    pallas_call x1, Pallas kernels, per_device(): pl.pallas_call(mix_kernel, out_shape=pltpu.VMEM((TOK, COLS), BF16), in_sp...  95.8 us

profile of v6, /device:TPU:1, one launch (start us, length us, event | category | flops | bytes accessed | tf_op | source)
XLA Modules:
  0.0 97.1 jit_solution(13921250526870662872)
XLA Ops:
  0.0 95.8 %shard_map.73 = bf16[1024,1024]{1,0:T(8,128)(2,1)S(1)} custom-call(bf16[3,512,1536]{2,1,0:T(8,128)(2,1)} %projections.1, bf16[128,1024]{1,0:T(8,128)(2,1)} %own_weight.1, s32[1,128]{1,0:T(1,128)} %bitcast.6, s32[1,128]{1,0:T(1,128)} %bitcast.7, f32[3,7,256]{2,1,0:T(8,128)} %bitcast.4, bf16[256,128]{1,0:T(8,128)(2,1)} %long_filter.1, f32[32,128]{1,0:T(8,128)} %bitcast.5), custom_call_target="tpu_custom_call" | custom-call | tf_op jit(solution)/shard_map/pallas_call | solution.py:641
  95.8 1.3 %copy.9 = bf16[1024,1024]{1,0:T(8,128)(2,1)} copy(bf16[1024,1024]{1,0:T(8,128)(2,1)S(1)} %shard_map.73) | data formatting | bytes 4194304
